TPU v7x, 32 devices: a whole 2x2x4 slice. The times are simulated.
32 devices in a mesh: ens: 2 (over y), tm: 4 (over x, core), lat: 4 (over z).
Axes of the slice: x: 2, y: 2, z: 4, core: 2. Of those that a mesh axis runs over, the one named last changes fastest.
Arguments:
- departures: float32 [8, 8, 69, 256], P(('ens', 'tm'), 'lat'), parts along dimension 0, may hold values from -6 to 6
- error_precision: float32 [8, 8, 69, 256], P(('ens', 'tm'), 'lat'), parts along dimension 0, may hold values from 0.5 to 4
- trajectory: bfloat16 [8, 8, 69, 256], P(('ens', 'tm'), 'lat'), parts along dimension 0, may hold values from -6 to 6
- conv_in: bfloat16 [3, 3, 128, 69], replicated, may hold values from -0.25 to 0.25
- conv_out: bfloat16 [3, 3, 69, 128], replicated, may hold values from -0.1875 to 0.1875
- hidden_bias: float32 [128], replicated, may hold values from -1 to 1
- step_counts: int32 [8], P(('ens', 'tm')), parts along dimension 0, may hold values from 1 to 2, as said below
- obs_tiles: int32 [8, 1024], P(('ens', 'tm'), 'lat'), parts along dimension 0, may hold values from 0 to 275
- obs_weights: float32 [8, 1024, 128], P(('ens', 'tm'), 'lat'), parts along dimension 0, may hold values from -0.5 to 0.5
- innovations: float32 [8, 1024], P(('ens', 'tm'), 'lat'), parts along dimension 0, may hold values from -6 to 6
- obs_precision: float32 [8, 1024], P(('ens', 'tm'), 'lat'), parts along dimension 0, may hold values from 0.5 to 4
Outputs:
- increment: float32 [8, 8, 69, 256], P(('ens', 'tm'), 'lat'), parts along dimension 0
- residual: float32 [8, 8, 69, 256], P(('ens', 'tm'), 'lat'), parts along dimension 0
There are 2 independent parts, one for each index of `ens`. A program takes and returns all parts, laid end to end along the dimension named above; an argument that names none is the same for every part. Nothing has to cross between parts.
Inputs may be any that keep to these rules, and one draw needn't show every extreme that they name: sub-window k runs step_counts[k] of its 2 hourly steps; some sub-window runs all of them.
All inputs are finite; a program needn't handle non-finite values.
Results may differ from a plain program's by a relative error of at most 0.02.
Values may be sent and summed in bfloat16 or wider, within the bound.
No kernel may reach another device: no remote copies, remote signals or barrier semaphores. Data moves between devices by JAX's collectives and lax.ppermute only.
A program may use at most 64 MiB of HBM per device.

v0:
```python
import functools

import jax
import jax.numpy as jnp
from jax import lax
from jax.experimental import pallas as pl
from jax.experimental.pallas import tpu as pltpu
from jax.sharding import PartitionSpec as P

TILE = 128
STEPS = 2
ITERS = 2
F32 = jnp.float32
BF16 = jnp.bfloat16


def padded_2(cells, sides, width):
    for axis, dim in sides:
        count = lax.axis_size(axis)
        ends = count - 1
        head = lax.slice_in_dim(cells, 0, width, axis=dim)
        tail = lax.slice_in_dim(cells, cells.shape[dim] - width, cells.shape[dim], axis=dim)
        cells = jnp.concatenate(
            [
                lax.ppermute(tail, axis, [(i, (i + 1) % count) for i in range(ends)]),
                cells,
                lax.ppermute(head, axis, [((i + 1) % count, i) for i in range(ends)]),
            ],
            axis=dim,
        )
    return cells


def from_behind(value, axis, steps):
    count = lax.axis_size(axis)
    leading, last = (max(0, -steps), min(count, count - steps))
    return lax.ppermute(value, axis, [(source, source + steps) for source in range(leading, last)])


def convolve_padded(padded, kernel):
    out_rows = padded.shape[0] - 2
    lon_len = padded.shape[2]
    wrapped = jnp.concatenate([padded[:, :, -1:], padded, padded[:, :, :1]], axis=2)
    accumulated = None
    for row_off in range(3):
        for col_off in range(3):
            window = wrapped[row_off : row_off + out_rows, :, col_off : col_off + lon_len]
            term = jnp.einsum(
                "oi,ril->rol", kernel[row_off, col_off], window, preferred_element_type=F32
            )
            accumulated = term if accumulated is None else accumulated + term
    return accumulated


def flipped(kernel):
    return jnp.transpose(kernel[::-1, ::-1], (0, 1, 3, 2))


def rim_wide(source):
    return padded_2(source, (("lat", 0),), 2)


def shift_up(source):
    return from_behind(source.astype(BF16), "tm", -1).astype(source.dtype)


def global_squares(source):
    return lax.psum(jnp.sum(source * source), ("tm", "lat"))


def halo_plan(
    departures,
    error_precision,
    trajectory,
    conv_in,
    conv_out,
    hidden_bias,
    step_counts,
    obs_tiles,
    obs_weights,
    innovations,
    obs_precision,
):
    precision = error_precision[0]
    own_count = step_counts[0]
    tile_index = obs_tiles[0]
    weights = obs_weights[0]
    innovation = innovations[0]
    obs_scale = obs_precision[0]
    back_in = flipped(conv_in)
    back_out = flipped(conv_out)
    trajectory_ext = padded_2(trajectory[0], (("lat", 0),), 1)
    gate_factor = (
        1.0 - jnp.tanh(convolve_padded(trajectory_ext, conv_in) + hidden_bias[:, None]) ** 2
    ).astype(BF16)
    gate_wide = padded_2(gate_factor, (("lat", 0),), 1)

    def one_step(current, first_kernel, second_kernel):
        widened = rim_wide(current.astype(BF16))
        hidden = (gate_wide.astype(F32) * convolve_padded(widened, first_kernel)).astype(BF16)
        return current + convolve_padded(hidden, second_kernel)

    def model(current, first_kernel, second_kernel):
        for step_index in range(STEPS):
            current = jnp.where(
                step_index < own_count, one_step(current, first_kernel, second_kernel), current
            )
        return current

    def observe_adjoint(scaled, like):
        tile_table = (
            jnp.zeros((like.size // TILE, TILE), F32)
            .at[tile_index]
            .add(weights * scaled[:, None])
        )
        return tile_table.reshape(like.shape)

    first_weighted = precision * departures[0]
    rhs = first_weighted + model(
        observe_adjoint(obs_scale * innovation, first_weighted) - shift_up(first_weighted),
        back_out,
        back_in,
    )
    increment = jnp.zeros_like(rhs)
    residual = rhs
    direction = rhs
    norm_now = global_squares(residual)
    for _ in range(ITERS):
        propagated = model(direction, conv_in, conv_out)
        earlier = from_behind(propagated.astype(BF16), "tm", 1).astype(F32)
        weighted = precision * (direction - earlier)
        picked = propagated.reshape(-1, TILE)[tile_index]
        observed = jnp.sum(picked * weights, axis=1)
        operator_image = weighted + model(
            observe_adjoint(obs_scale * observed, direction) - shift_up(weighted),
            back_out,
            back_in,
        )
        curvature = lax.psum(jnp.sum(direction * operator_image), ("tm", "lat"))
        step_length = norm_now / curvature
        increment = increment + step_length * direction
        residual = residual - step_length * operator_image
        norm_next = global_squares(residual)
        direction = residual + norm_next / norm_now * direction
        norm_now = norm_next
    return (increment[None], residual[None])


BANDS = 4
ROWS = 2 * BANDS
CHAN = 72
CHAN_IN = 80
TAPS = 256
PAIR = 2 * CHAN
SLOTS = 4 * CHAN
OBS_ROWS = 144


def row_of(ref, row):
    return ref[row // 2, (row % 2) * CHAN : (row % 2 + 1) * CHAN, :]


def taps_of(row):
    zeros = jnp.zeros((CHAN_IN - CHAN, row.shape[1]), F32)
    right = pltpu.roll(row, 1, axis=1)
    left = pltpu.roll(row, row.shape[1] - 1, axis=1)
    return jnp.concatenate([right, zeros, row, zeros, left, zeros], axis=0).astype(BF16)


def clear_taps(taps):
    used = 3 * CHAN_IN
    taps[:, used:, :] = jnp.zeros((ROWS, TAPS - used, taps.shape[2]), BF16)


def conv_rows(field, w_in, taps, emit):
    for row in range(ROWS):
        taps[row, : 3 * CHAN_IN] = taps_of(row_of(field, row))
    for row in range(ROWS):
        low, high = max(row - 1, 0), min(row + 2, ROWS)
        stacked = taps[low:high].reshape((high - low) * TAPS, taps.shape[2])
        skip = (low - (row - 1)) * TAPS
        weights = w_in[:, skip : skip + (high - low) * TAPS]
        emit(row, jnp.dot(weights, stacked, preferred_element_type=F32))


def model_steps(field, gate, w_in, w_out, taps, hidden, count):
    clear_taps(taps)
    hidden[0] = jnp.zeros(hidden.shape[1:], BF16)
    hidden[ROWS + 1] = jnp.zeros(hidden.shape[1:], BF16)

    def gated(row, value):
        hidden[row + 1] = (gate[row].astype(F32) * value).astype(BF16)

    def one_step(_, carry):
        conv_rows(field, w_in, taps, gated)
        for pair in range(BANDS):
            stacked = hidden[2 * pair : 2 * pair + 4].reshape(-1, hidden.shape[2])
            part = jnp.dot(w_out[...], stacked, preferred_element_type=F32)
            lon = part.shape[1]
            for row in range(2):
                tap = [part[(3 * row + b) * CHAN : (3 * row + b + 1) * CHAN] for b in range(3)]
                spread = pltpu.roll(tap[0], 1, axis=1) + tap[1] + pltpu.roll(tap[2], lon - 1, axis=1)
                at = row * CHAN
                field[pair, at : at + CHAN, :] = field[pair, at : at + CHAN, :] + spread
        return carry

    lax.fori_loop(0, jnp.minimum(count, STEPS), one_step, 0)


def split_16(value):
    high = value.astype(BF16)
    low = (value - high.astype(F32)).astype(BF16)
    return high, low


def obs_of(obs):
    weights = jnp.concatenate([obs[:TILE, :TILE], obs[:TILE, TILE:]], axis=0)
    extra = obs[TILE:, :].astype(F32)
    return weights, 2.0 * extra[0:1] + extra[1:2], extra[2:3], extra[3:4]


def one_hot_t(slot):
    iota = lax.broadcasted_iota(jnp.int32, (SLOTS, 2 * TILE), 0).astype(F32)
    return (iota == slot).astype(F32)


def one_hot(slot):
    columns = [
        jnp.transpose(jnp.broadcast_to(slot[:, half * TILE : (half + 1) * TILE], (TILE, TILE)))[:, :1]
        for half in range(2)
    ]
    column = jnp.concatenate(columns, axis=0)
    iota = lax.broadcasted_iota(jnp.int32, (2 * TILE, SLOTS), 1).astype(F32)
    return (iota == column).astype(F32)


def band_slots(band):
    return jnp.concatenate(
        [
            band[row * CHAN : (row + 1) * CHAN, half * TILE : (half + 1) * TILE]
            for row in range(2)
            for half in range(2)
        ],
        axis=0,
    )


def slots_band(slots):
    return jnp.concatenate(
        [
            jnp.concatenate(
                [slots[(2 * row + half) * CHAN : (2 * row + half + 1) * CHAN] for half in range(2)],
                axis=1,
            )
            for row in range(2)
        ],
        axis=0,
    )


def gate_kernel(b0, b1, b2, b3, w_in, bias, gate, field, taps):
    me = lax.axis_index("lat")
    for shift, block in enumerate((b0, b1, b2, b3)):
        field[me ^ shift] = block[0].astype(F32)
    clear_taps(taps)

    def emit(row, value):
        squashed = jnp.tanh(value + bias[...])
        gate[row] = (1.0 - squashed * squashed).astype(BF16)

    conv_rows(field, w_in, taps, emit)


def rhs_kernel(
    counts, y0, y1, y2, y3, later, b0, b1, b2, b3, gate, w_in, w_out, out, out_b, field, taps, hidden
):
    me = lax.axis_index("lat")
    more = lax.axis_index("tm") < lax.axis_size("tm") - 1
    for shift, block in enumerate((b0, b1, b2, b3)):
        weights, slot, high, low = obs_of(block[1])
        hot = one_hot_t(slot)
        both = jnp.concatenate([hot * high, hot * low], axis=1).astype(BF16)
        slots = jnp.dot(
            both, jnp.concatenate([weights, weights], axis=0), preferred_element_type=F32
        )
        next_y = jnp.where(more, later[shift].astype(F32), 0.0)
        field[me ^ shift] = slots_band(slots) - next_y
    model_steps(field, gate, w_in, w_out, taps, hidden, counts[0])
    for shift, block in enumerate((y0, y1, y2, y3)):
        total = field[me ^ shift] + block[...].astype(F32)
        out[me ^ shift] = total
        out_b[me ^ shift] = total.astype(BF16)


def forward_kernel(counts, start, gate, w_in, w_out, out, out_b, taps, hidden):
    out[...] = start[...]
    model_steps(out, gate, w_in, w_out, taps, hidden, counts[0])
    out_b[...] = out[...].astype(BF16)


def observe_kernel(z, b0, b1, b2, b3, out, energy):
    me = lax.axis_index("lat")
    squares = jnp.zeros((1, 1), F32)
    for shift, block in enumerate((b0, b1, b2, b3)):
        weights, slot, _, _ = obs_of(block[1])
        weights = weights.astype(F32)
        high, low = split_16(band_slots(z[me ^ shift]))
        both = jnp.concatenate([high, low], axis=1)
        picked = jnp.dot(one_hot(slot).astype(BF16), both, preferred_element_type=F32)
        picked = picked[:, :TILE] + picked[:, TILE:]
        scaled = jnp.sum(picked * weights, axis=1, keepdims=True)
        squares = squares + jnp.sum(scaled * scaled, axis=0, keepdims=True)
        high, low = split_16(weights * scaled)
        both = jnp.concatenate([high, low], axis=1)
        slots = jnp.dot(one_hot_t(slot).astype(BF16), both, preferred_element_type=F32)
        out[me ^ shift] = slots_band(slots[:, :TILE] + slots[:, TILE:])
    energy[...] = jnp.broadcast_to(squares, energy.shape)


def adjoint_kernel(
    counts, observed, z, later, precision, gate, w_in, w_out, out, taps, hidden
):
    me = lax.axis_index("lat")
    more = lax.axis_index("tm") < lax.axis_size("tm") - 1
    for shift in range(BANDS):
        at = me ^ shift
        weight = jnp.where(more, precision[shift].astype(F32), 0.0)
        out[at] = observed[at] - weight * (later[at].astype(F32) - z[at])
    model_steps(out, gate, w_in, w_out, taps, hidden, counts[0])


def image_of(at, tm_first, block, start, earlier, adjoint):
    before = jnp.where(tm_first, 0.0, earlier[at].astype(F32))
    return block.astype(F32) * (start[at] - before) + adjoint[at]


def image_kernel(start, earlier, adjoint, p0, p1, p2, p3, out, out_b):
    me = lax.axis_index("lat")
    tm_first = lax.axis_index("tm") == 0
    for shift, block in enumerate((p0, p1, p2, p3)):
        at = me ^ shift
        total = image_of(at, tm_first, block[...], start, earlier, adjoint)
        out[at] = total
        out_b[at] = total.astype(BF16)


def products_kernel(first, second, z, later, precision, p0, p1, p2, p3, energy, dots):
    me = lax.axis_index("lat")
    tm_first = lax.axis_index("tm") == 0
    more = lax.axis_index("tm") < lax.axis_size("tm") - 1
    sums = [jnp.zeros((1, first.shape[2]), F32) for _ in range(4)]
    for shift, block in enumerate((p0, p1, p2, p3)):
        at = me ^ shift
        r0, v1 = first[at], second[at]
        misfit = later[at].astype(F32) - z[at]
        weight = jnp.where(more, precision[shift].astype(F32), 0.0)
        initial = jnp.where(tm_first, block[...].astype(F32), 0.0)
        terms = (r0 * r0, r0 * v1, v1 * v1, weight * misfit * misfit + initial * v1 * v1)
        sums = [total + jnp.sum(term, axis=0, keepdims=True) for total, term in zip(sums, terms)]
    for j, total in enumerate(sums):
        value = jnp.broadcast_to(jnp.sum(total, axis=1, keepdims=True), (1, TILE))
        dots[j : j + 1, :] = value + energy[:1, :] if j == 3 else value
    dots[4:8, :] = jnp.zeros((4, TILE), F32)


def finish_kernel(d0, d1, d2, d3, first, second, earlier, adjoint, p0, inc, res):
    me = lax.axis_index("lat")
    tm_first = lax.axis_index("tm") == 0
    chan, _, lon = inc.shape
    total = (d0[...] + d1[...]) + (d2[...] + d3[...])
    rr0, c0, g11, g12 = [total[j : j + 1, :1] for j in range(4)]
    a0 = rr0 / c0
    rr1 = rr0 - 2.0 * a0 * c0 + a0 * a0 * g11
    beta = rr1 / rr0
    grow = 1.0 + beta
    c1 = grow * grow * c0 - 2.0 * grow * a0 * g11 + a0 * a0 * g12
    a1 = rr1 / c1
    wide = lambda value: jnp.broadcast_to(value, (chan, lon))
    along, cross = wide(a0 + a1 * grow), wide(a1 * a0)
    image = image_of(me, tm_first, p0[...], second, earlier, adjoint)
    r0_own, v1_own = first[me], second[me]
    for row in range(2):
        at = row * CHAN
        r0, v1, v2 = [field[at : at + chan] for field in (r0_own, v1_own, image)]
        inc[:, row, :] = along * r0 - cross * v1
        res[:, row, :] = r0 - along * v1 + cross * v2


VMEM = pl.BlockSpec(memory_space=pltpu.VMEM)
SMEM = pl.BlockSpec(memory_space=pltpu.SMEM)


def call(kernel, name, ins, outs, scratch=(), scalars=0):
    specs = [SMEM] * scalars + [VMEM] * (len(ins) - scalars)
    return pl.pallas_call(
        kernel,
        name=name,
        out_shape=outs,
        in_specs=specs,
        out_specs=[VMEM] * len(outs),
        scratch_shapes=list(scratch),
        compiler_params=pltpu.CompilerParams(vmem_limit_bytes=48 << 20),
        cost_estimate=pl.CostEstimate(flops=1, bytes_accessed=1, transcendentals=0),
    )(*ins)


def stack_in(kernel):
    rows, cols, out_c, in_c = kernel.shape
    padded = jnp.pad(kernel, ((0, 0), (0, 0), (0, 0), (0, CHAN_IN - in_c)))
    block = jnp.transpose(padded, (2, 0, 1, 3)).reshape(out_c, rows, cols * CHAN_IN)
    block = jnp.pad(block, ((0, 0), (0, 0), (0, TAPS - cols * CHAN_IN)))
    return block.reshape(out_c, rows * TAPS)


def stack_out(kernel):
    rows, cols, out_c, in_c = kernel.shape
    padded = jnp.pad(kernel, ((0, 0), (0, 0), (0, CHAN - out_c), (0, 0)))
    none = jnp.zeros_like(padded[0])
    tap = lambda row_off: padded[row_off] if 0 <= row_off < rows else none
    blocks = [jnp.concatenate([tap(t - m) for t in range(4)], axis=-1) for m in range(2)]
    return jnp.concatenate(blocks, axis=0).reshape(2 * cols * CHAN, 4 * in_c)


def as_band(cells):
    rows, chan, lon = cells.shape
    return jnp.pad(cells.astype(BF16), ((0, 0), (0, CHAN - chan), (0, 0))).reshape(PAIR, lon)


def swap(block, shift):
    count = lax.axis_size("lat")
    return lax.ppermute(block, "lat", [(i, i ^ shift) for i in range(count)])


def by_partner(value):
    far = swap(value, 2)
    return [value, swap(value, 1), far, swap(far, 1)]


def along_tm(value, step):
    count = lax.axis_size("tm")
    return lax.ppermute(value, "tm", [(i, (i + step) % count) for i in range(count)])


def row_plan(
    departures,
    error_precision,
    trajectory,
    conv_in,
    conv_out,
    hidden_bias,
    step_counts,
    obs_tiles,
    obs_weights,
    innovations,
    obs_precision,
):
    _, rows, chan, lon = departures.shape
    hid = conv_in.shape[2]
    shape = lambda *dims: jax.ShapeDtypeStruct(dims, F32)
    shape_b = lambda *dims: jax.ShapeDtypeStruct(dims, BF16)
    whole, whole_b = shape(BANDS, PAIR, lon), shape_b(BANDS, PAIR, lon)

    root = jnp.sqrt(obs_precision[0])
    tiles = obs_tiles[0]
    per_row = 2 * chan
    slot = (2 * (tiles // per_row) + tiles % 2) * CHAN + (tiles // 2) % chan
    innov_high, innov_low = split_16(root * innovations[0])
    table = lambda value: value.astype(BF16).reshape(1, 2 * TILE)
    weights = (obs_weights[0] * root[:, None]).astype(BF16)
    obs_own = jnp.concatenate(
        [
            jnp.concatenate([weights[:TILE], weights[TILE:]], axis=1),
            table(slot // 2),
            table(slot % 2),
            table(innov_high),
            table(innov_low),
            jnp.zeros((OBS_ROWS - TILE - 4, 2 * TILE), BF16),
        ],
        axis=0,
    )
    both_own = jnp.stack([as_band(trajectory[0]), obs_own])
    prec_own = as_band(error_precision[0])

    y_all = by_partner(as_band(error_precision[0] * departures[0]))
    b_all = by_partner(both_own)
    p_all = by_partner(prec_own)
    y_later = along_tm(jnp.stack(y_all), -1)
    p_later = along_tm(jnp.stack(p_all), -1)

    fore_in, fore_out = stack_in(conv_in), stack_out(conv_out)
    back_in, back_out = stack_in(flipped(conv_out)), stack_out(flipped(conv_in))
    taps = pltpu.VMEM((ROWS, TAPS, lon), BF16)
    hidden = pltpu.VMEM((ROWS + 2, hid, lon), BF16)
    field = pltpu.VMEM((BANDS, PAIR, lon), F32)

    (gate,) = call(
        gate_kernel,
        "gate",
        (*b_all, fore_in, hidden_bias[:, None]),
        [shape_b(ROWS, hid, lon)],
        [field, taps],
    )
    r0, r0_b = call(
        rhs_kernel,
        "rhs",
        (step_counts, *y_all, y_later, *b_all, gate, back_in, back_out),
        [whole, whole_b],
        [field, taps, hidden],
        1,
    )

    def to_misfits(start, start_b):
        later = along_tm(start_b, -1)
        z, z_b = call(
            forward_kernel,
            "forward",
            (step_counts, start, gate, fore_in, fore_out),
            [whole, whole_b],
            [taps, hidden],
            1,
        )
        observed, energy = call(observe_kernel, "observe", (z, *b_all), [whole, shape(8, TILE)])
        return along_tm(z_b, 1), later, z, observed, energy

    def adjoint_of(later, z, observed):
        return call(
            adjoint_kernel,
            "adjoint",
            (step_counts, observed, z, later, p_later, gate, back_in, back_out),
            [whole],
            [taps, hidden],
            1,
        )[0]

    earlier, later, z, observed, _ = to_misfits(r0, r0_b)
    adjoint = adjoint_of(later, z, observed)
    v1, v1_b = call(image_kernel, "image", (r0, earlier, adjoint, *p_all), [whole, whole_b])
    earlier, later, z, observed, energy = to_misfits(v1, v1_b)
    (dots,) = call(
        products_kernel,
        "products",
        (r0, v1, z, later, p_later, *p_all, energy),
        [shape(8, TILE)],
    )
    count = lax.axis_size("tm")
    parts = [dots] + [
        lax.ppermute(dots, "tm", [(i, i ^ step) for i in range(count)]) for step in range(1, count)
    ]
    observed, _ = lax.optimization_barrier((observed, dots))
    adjoint = adjoint_of(later, z, observed)
    inc, res = call(
        finish_kernel,
        "finish",
        (*parts, r0, v1, earlier, adjoint, p_all[0]),
        [shape(chan, rows, lon)] * 2,
    )
    return (jnp.transpose(inc, (1, 0, 2))[None], jnp.transpose(res, (1, 0, 2))[None])


def solution(mesh):
    in_specs = (
        P(("ens", "tm"), "lat", None, None),
        P(("ens", "tm"), "lat", None, None),
        P(("ens", "tm"), "lat", None, None),
        P(),
        P(),
        P(),
        P(("ens", "tm")),
        P(("ens", "tm"), "lat"),
        P(("ens", "tm"), "lat", None),
        P(("ens", "tm"), "lat"),
        P(("ens", "tm"), "lat"),
    )
    out_specs = (P(("ens", "tm"), "lat", None, None), P(("ens", "tm"), "lat", None, None))
    plan = row_plan if mesh.shape["lat"] == BANDS and mesh.shape["tm"] == 4 else halo_plan
    return jax.shard_map(plan, mesh=mesh, in_specs=in_specs, out_specs=out_specs, check_vma=False)
```

profile of v0, /device:TPU:0, one launch (start us, length us, event | category | flops | bytes accessed | tf_op | source)
XLA Modules:
  0.0 55.4 jit_solution(7233411962296287163)
XLA Ops:
  0.6 1.2 %convert_bitcast_fusion = (bf16[2,69,256]{2,0,1:T(2,128)(2,1)S(1)}, bf16[2,69,256]{2,0,1:T(2,128)(2,1)S(1)}) fusion(f32[1,2,69,256]{3,1,2,0:T(2,128)} %param.12, f32[1,2,69,256]{3,1,2,0:T(2,128)} %param.11), kind=kLoop, calls=%fused_computation.25 | loop fusion | flops 105984 | bytes 423936 | tf_op jit(solution)/shard_map/convert_element_type | solution.py:426
  1.8 4.1 %collective-permute-start.1 = (bf16[144,256]{1,0:T(8,128)(2,1)S(1)}, bf16[144,256]{1,0:T(8,128)(2,1)S(1)}, u32[]{:S(2)}, u32[]{:S(2)}) collective-permute-start(bf16[144,256]{1,0:T(8,128)(2,1)S(1)} %bitcast.66), channel_id=1, source_target_pairs={{0,2},{1,3},{2,0},{3,1},{4,6},{5,7},{6,4},{7,5},{8,10},{9,11},{10,... | collective-permute-start | bytes 221192 | tf_op jit(solution)/shard_map/ppermute | solution.py:431
  5.9 1.6 %collective-permute-start = (bf16[144,256]{1,0:T(8,128)(2,1)S(1)}, bf16[144,256]{1,0:T(8,128)(2,1)S(1)}, u32[]{:S(2)}, u32[]{:S(2)}) collective-permute-start(bf16[144,256]{1,0:T(8,128)(2,1)S(1)} %bitcast.67), channel_id=1, source_target_pairs={{0,1},{1,0},{2,3},{3,2},{4,5},{5,4},{6,7},{7,6},{8,9},{9,8},{10,11... | collective-permute-start | bytes 221192 | tf_op jit(solution)/shard_map/ppermute | solution.py:431
  7.6 0.4 collective-permute-start.10
  8.0 0.2 collective-permute-start.9
  8.5 0.9 %copy-done.3 = bf16[1,2,69,256]{3,1,2,0:T(2,128)(2,1)S(1)} copy-done((bf16[1,2,69,256]{3,1,2,0:T(2,128)(2,1)S(1)}, bf16[1,2,69,256]{3,1,2,0:T(2,128)(2,1)}, u32[]{:S(2)}) %copy-start.3) | copy-done | bytes 70680
  9.7 2.8 %collective-permute-start.5 = (bf16[2,144,256]{2,1,0:T(8,128)(2,1)S(1)}, bf16[2,144,256]{2,1,0:T(8,128)(2,1)S(1)}, u32[]{:S(2)}, u32[]{:S(2)}) collective-permute-start(bf16[2,144,256]{2,1,0:T(8,128)(2,1)S(1)} %pad_maximum_fusion.6.b0), channel_id=1, source_target_pairs={{0,2},{1,3},{2,0},{3,1},{4,6},{5,7},{6,4},{7,5},{8,10},{9,11},{10,... | collective-permute-start | bytes 442376 | tf_op jit(solution)/shard_map/ppermute | solution.py:431
  12.5 1.6 %collective-permute-start.2 = (bf16[144,256]{1,0:T(8,128)(2,1)S(1)}, bf16[144,256]{1,0:T(8,128)(2,1)S(1)}, u32[]{:S(2)}, u32[]{:S(2)}) collective-permute-start(bf16[144,256]{1,0:T(8,128)(2,1)S(1)} %collective-permute-done.1.y2), channel_id=1, source_target_pairs={{0,1},{1,0},{2,3},{3,2},{4,5},{5,4},{6,7},{7,6},{8,9},{9,8},{10,11... | collective-permute-start | bytes 221192 | tf_op jit(solution)/shard_map/ppermute | solution.py:431
  14.2 0.5 collective-permute-start.4
  14.7 5.7 %collective-permute-done.2.y3 = bf16[144,256]{1,0:T(8,128)(2,1)S(1)} collective-permute-done((bf16[144,256]{1,0:T(8,128)(2,1)S(1)}, bf16[144,256]{1,0:T(8,128)(2,1)S(1)}, u32[]{:S(2)}, u32[]{:S(2)}) %collective-permute-start.2) | collective-permute-done | bytes 73760 | tf_op jit(solution)/shard_map/ppermute | solution.py:431
  20.6 0.5 collective-permute-start.11
  21.1 1.6 %collective-permute-start.6 = (bf16[2,144,256]{2,1,0:T(8,128)(2,1)S(1)}, bf16[2,144,256]{2,1,0:T(8,128)(2,1)S(1)}, u32[]{:S(2)}, u32[]{:S(2)}) collective-permute-start(bf16[2,144,256]{2,1,0:T(8,128)(2,1)S(1)} %collective-permute-done.5.b2), channel_id=1, source_target_pairs={{0,1},{1,0},{2,3},{3,2},{4,5},{5,4},{6,7},{7,6},{8,9},{9,8},{10,11... | collective-permute-start | bytes 442376 | tf_op jit(solution)/shard_map/ppermute | solution.py:431
  23.3 0.6 %copy-done.7 = f32[128]{0:T(128)S(1)} copy-done((f32[128]{0:T(128)S(1)}, f32[128]{0:T(128)}, u32[]{:S(2)}) %copy-start.7) | copy-done | bytes 536
  24.5 1.2 %collective-permute-done.11.p3 = bf16[144,256]{1,0:T(8,128)(2,1)S(1)} collective-permute-done((bf16[144,256]{1,0:T(8,128)(2,1)S(1)}, bf16[144,256]{1,0:T(8,128)(2,1)S(1)}, u32[]{:S(2)}, u32[]{:S(2)}) %collective-permute-start.11) | collective-permute-done | bytes 73760 | tf_op jit(solution)/shard_map/ppermute | solution.py:431
  25.7 0.5 collective-permute-start.12
  26.2 2.3 %collective-permute-done.6.b3 = bf16[2,144,256]{2,1,0:T(8,128)(2,1)S(1)} collective-permute-done((bf16[2,144,256]{2,1,0:T(8,128)(2,1)S(1)}, bf16[2,144,256]{2,1,0:T(8,128)(2,1)S(1)}, u32[]{:S(2)}, u32[]{:S(2)}) %collective-permute-start.6) | collective-permute-done | bytes 147488 | tf_op jit(solution)/shard_map/ppermute | solution.py:431
  28.4 0.7 %gate.1 = bf16[8,128,256]{2,1,0:T(8,128)(2,1)S(1)} custom-call(bf16[2,144,256]{2,1,0:T(8,128)(2,1)S(1)} %pad_maximum_fusion.6.b0, bf16[2,144,256]{2,1,0:T(8,128)(2,1)S(1)} %collective-permute-done.4.b1, bf16[2,144,256]{2,1,0:T(8,128)(2,1)S(1)} %collective-permute-done.5.b2, bf16[2,144,256]{2,1,0:T(8,128)(2,1)S(1)} %collective-permute-done.6.b3, ...), custom_call_target="tpu_custom_call" | custom-call | flops 1 | bytes 1 | tf_op jit(solution)/shard_map/gate/pallas_call | solution.py:395
  29.1 1.8 %rhs.1 = (f32[4,144,256]{2,1,0:T(8,128)S(1)}, bf16[4,144,256]{2,1,0:T(8,128)(2,1)S(1)}) custom-call(s32[1]{0:T(128)S(6)} %copy.36.counts, bf16[144,256]{1,0:T(8,128)(2,1)S(1)} %bitcast.69, bf16[144,256]{1,0:T(8,128)(2,1)S(1)} %collective-permute-done.y1, bf16[144,256]{1,0:T(8,128)(2,1)S(1)} %collective-permute-done.1.y2, ...), custom_call_target="tpu_custom_call" | custom-call | flops 1 | bytes 1 | tf_op jit(solution)/shard_map/rhs/pallas_call | solution.py:395
  30.9 0.9 %collective-permute-start.8 = (bf16[4,144,256]{2,1,0:T(8,128)(2,1)S(1)}, bf16[4,144,256]{2,1,0:T(8,128)(2,1)S(1)}, u32[]{:S(2)}, u32[]{:S(2)}) collective-permute-start(bf16[4,144,256]{2,1,0:T(8,128)(2,1)S(1)} %get-tuple-element.20), channel_id=1, source_target_pairs={{0,12},{4,0},{8,4},{12,8},{1,13},{5,1},{9,5},{13,9},{2,14},{6,2},{... | collective-permute-start | bytes 884744 | tf_op jit(solution)/shard_map/ppermute | solution.py:441
  31.8 1.3 %forward.2 = (f32[4,144,256]{2,1,0:T(8,128)S(1)}, bf16[4,144,256]{2,1,0:T(8,128)(2,1)S(1)}) custom-call(s32[1]{0:T(128)S(6)} %copy.36.counts, f32[4,144,256]{2,1,0:T(8,128)S(1)} %get-tuple-element.16.start.first, bf16[8,128,256]{2,1,0:T(8,128)(2,1)S(1)} %gate.1, bf16[128,768]{1,0:T(8,128)(2,1)S(1)} %copy.24.w_in, bf16[432,512]{1,0:T(8,128)(2,1)S(1)} %bitcast.58), custom_call_target="tpu_custom_call" | custom-call | flops 1 | bytes 1 | tf_op jit(solution)/shard_map/forward/pallas_call | solution.py:395
  33.1 2.6 %observe.2 = (f32[4,144,256]{2,1,0:T(8,128)S(1)}, f32[8,128]{1,0:T(8,128)}) custom-call(f32[4,144,256]{2,1,0:T(8,128)S(1)} %get-tuple-element.18.z, bf16[2,144,256]{2,1,0:T(8,128)(2,1)S(1)} %pad_maximum_fusion.6.b0, bf16[2,144,256]{2,1,0:T(8,128)(2,1)S(1)} %collective-permute-done.4.b1, bf16[2,144,256]{2,1,0:T(8,128)(2,1)S(1)} %collective-permute-done.5.b2, ...), custom_call_target="tpu_custom_call" | custom-call | flops 1 | bytes 1 | tf_op jit(solution)/shard_map/observe/pallas_call | solution.py:395
  35.7 0.3 collective-permute-done.8.later
  36.0 1.4 %adjoint.2 = f32[4,144,256]{2,1,0:T(8,128)S(1)} custom-call(s32[1]{0:T(128)S(6)} %copy.36.counts, f32[4,144,256]{2,1,0:T(8,128)S(1)} %get-tuple-element.19.observed, f32[4,144,256]{2,1,0:T(8,128)S(1)} %get-tuple-element.18.z, bf16[4,144,256]{2,1,0:T(8,128)(2,1)S(1)} %collective-permute-done.8.later, ...), custom_call_target="tpu_custom_call" | custom-call | flops 1 | bytes 1 | tf_op jit(solution)/shard_map/adjoint/pallas_call | solution.py:395
  37.4 4.1 %collective-permute-done.7.earlier = bf16[4,144,256]{2,1,0:T(8,128)(2,1)S(1)} collective-permute-done((bf16[4,144,256]{2,1,0:T(8,128)(2,1)S(1)}, bf16[4,144,256]{2,1,0:T(8,128)(2,1)S(1)}, u32[]{:S(2)}, u32[]{:S(2)}) %collective-permute-start.7) | collective-permute-done | bytes 294944 | tf_op jit(solution)/shard_map/ppermute | solution.py:441
  41.8 1.3 %forward.3 = (f32[4,144,256]{2,1,0:T(8,128)S(1)}, bf16[4,144,256]{2,1,0:T(8,128)(2,1)S(1)}) custom-call(s32[1]{0:T(128)S(6)} %copy.36.counts, f32[4,144,256]{2,1,0:T(8,128)S(1)} %get-tuple-element.21.start.second, bf16[8,128,256]{2,1,0:T(8,128)(2,1)S(1)} %gate.1, bf16[128,768]{1,0:T(8,128)(2,1)S(1)} %copy.24.w_in, bf16[432,512]{1,0:T(8,128)(2,1)S(1)} %bitcast.59), custom_call_target="tpu_custom_call" | custom-call | flops 1 | bytes 1 | tf_op jit(solution)/shard_map/forward/pallas_call | solution.py:395
  43.0 0.7 %collective-permute-start.17 = (bf16[4,144,256]{2,1,0:T(8,128)(2,1)S(1)}, bf16[4,144,256]{2,1,0:T(8,128)(2,1)S(1)}, u32[]{:S(2)}, u32[]{:S(2)}) collective-permute-start(bf16[4,144,256]{2,1,0:T(8,128)(2,1)S(1)} %get-tuple-element.25), channel_id=1, source_target_pairs={{0,4},{4,8},{8,12},{12,0},{1,5},{5,9},{9,13},{13,1},{2,6},{6,10},{... | collective-permute-start | bytes 884744 | tf_op jit(solution)/shard_map/ppermute | solution.py:441
  43.8 2.2 %observe.3 = (f32[4,144,256]{2,1,0:T(8,128)S(1)}, f32[8,128]{1,0:T(8,128)S(1)}) custom-call(f32[4,144,256]{2,1,0:T(8,128)S(1)} %get-tuple-element.22.z, bf16[2,144,256]{2,1,0:T(8,128)(2,1)S(1)} %pad_maximum_fusion.6.b0, bf16[2,144,256]{2,1,0:T(8,128)(2,1)S(1)} %collective-permute-done.4.b1, bf16[2,144,256]{2,1,0:T(8,128)(2,1)S(1)} %collective-permute-done.5.b2, ...), custom_call_target="tpu_custom_call" | custom-call | flops 1 | bytes 1 | tf_op jit(solution)/shard_map/observe/pallas_call | solution.py:395
  46.0 0.6 products.1.d0
  46.5 1.9 %collective-permute-start.16 = (f32[8,128]{1,0:T(8,128)S(1)}, f32[8,128]{1,0:T(8,128)S(1)}, u32[]{:S(2)}, u32[]{:S(2)}) collective-permute-start(f32[8,128]{1,0:T(8,128)S(1)} %products.1.d0), channel_id=1, source_target_pairs={{0,12},{4,8},{8,4},{12,0},{1,13},{5,9},{9,5},{13,1},{2,14},{6,10},... | collective-permute-start | bytes 12296 | tf_op jit(solution)/shard_map/ppermute | solution.py:547
  48.5 4.4 %collective-permute-start.15 = (f32[8,128]{1,0:T(8,128)S(1)}, f32[8,128]{1,0:T(8,128)S(1)}, u32[]{:S(2)}, u32[]{:S(2)}) collective-permute-start(f32[8,128]{1,0:T(8,128)S(1)} %products.1.d0), channel_id=1, source_target_pairs={{0,8},{4,12},{8,0},{12,4},{1,9},{5,13},{9,1},{13,5},{2,10},{6,14},... | collective-permute-start | bytes 12296 | tf_op jit(solution)/shard_map/ppermute | solution.py:547
  52.9 1.4 %adjoint.3 = f32[4,144,256]{2,1,0:T(8,128)S(1)} custom-call(s32[1]{0:T(128)S(6)} %copy.36.counts, f32[4,144,256]{2,1,0:T(8,128)S(1)} %get-tuple-element.27.observed, f32[4,144,256]{2,1,0:T(8,128)S(1)} %get-tuple-element.22.z, bf16[4,144,256]{2,1,0:T(8,128)(2,1)S(1)} %collective-permute-done.13.later, ...), custom_call_target="tpu_custom_call" | custom-call | flops 1 | bytes 1 | tf_op jit(solution)/shard_map/adjoint/pallas_call | solution.py:395
  54.5 0.9 %finish.1 = (f32[69,2,256]{2,1,0:T(2,128)}, f32[69,2,256]{2,1,0:T(2,128)}) custom-call(f32[8,128]{1,0:T(8,128)S(1)} %products.1.d0, f32[8,128]{1,0:T(8,128)S(1)} %collective-permute-done.14.d1, f32[8,128]{1,0:T(8,128)S(1)} %collective-permute-done.15.d2, f32[8,128]{1,0:T(8,128)S(1)} %collective-permute-done.16.d3, ...), custom_call_target="tpu_custom_call" | custom-call | flops 1 | bytes 1 | tf_op jit(solution)/shard_map/finish/pallas_call | solution.py:395
  (61 shorter events, 1.9 us)
Async XLA Ops:
  1.8 10.6 %collective-permute-start.1 = (bf16[144,256]{1,0:T(8,128)(2,1)S(1)}, bf16[144,256]{1,0:T(8,128)(2,1)S(1)}, u32[]{:S(2)}, u32[]{:S(2)}) collective-permute-start(bf16[144,256]{1,0:T(8,128)(2,1)S(1)} %bitcast.66), channel_id=1, source_target_pairs={{0,2},{1,3},{2,0},{3,1},{4,6},{5,7},{6,4},{7,5},{8,10},{9,11},{10,... | collective-permute-start | bytes 221192 | tf_op jit(solution)/shard_map/ppermute | solution.py:431
  5.9 8.2 %collective-permute-start = (bf16[144,256]{1,0:T(8,128)(2,1)S(1)}, bf16[144,256]{1,0:T(8,128)(2,1)S(1)}, u32[]{:S(2)}, u32[]{:S(2)}) collective-permute-start(bf16[144,256]{1,0:T(8,128)(2,1)S(1)} %bitcast.67), channel_id=1, source_target_pairs={{0,1},{1,0},{2,3},{3,2},{4,5},{5,4},{6,7},{7,6},{8,9},{9,8},{10,11... | collective-permute-start | bytes 221192 | tf_op jit(solution)/shard_map/ppermute | solution.py:431
  7.5 0.9 %copy-start.2 = (f32[1,256,128]{2,1,0:T(8,128)S(1)}, f32[1,256,128]{2,1,0:T(8,128)}, u32[]{:S(2)}) copy-start(f32[1,256,128]{2,1,0:T(8,128)} %param.19) | copy-start | bytes 393220
  7.5 0.7 %copy-start.6 = (s32[1,256]{1,0:T(1,128)S(1)}, s32[1,256]{1,0:T(1,128)}, u32[]{:S(2)}) copy-start(s32[1,256]{1,0:T(1,128)} %param.18) | copy-start | bytes 3076
  7.6 0.7 %copy-start.4 = (f32[1,256]{1,0:T(1,128)S(1)}, f32[1,256]{1,0:T(1,128)}, u32[]{:S(2)}) copy-start(f32[1,256]{1,0:T(1,128)} %param.20) | copy-start | bytes 3076
  7.6 0.7 %copy-start.5 = (f32[1,256]{1,0:T(1,128)S(1)}, f32[1,256]{1,0:T(1,128)}, u32[]{:S(2)}) copy-start(f32[1,256]{1,0:T(1,128)} %param.21) | copy-start | bytes 3076
  7.6 13.0 %collective-permute-start.10 = (bf16[144,256]{1,0:T(8,128)(2,1)S(1)}, bf16[144,256]{1,0:T(8,128)(2,1)S(1)}, u32[]{:S(2)}, u32[]{:S(2)}) collective-permute-start(bf16[144,256]{1,0:T(8,128)(2,1)S(1)} %bitcast.60), channel_id=1, source_target_pairs={{0,2},{1,3},{2,0},{3,1},{4,6},{5,7},{6,4},{7,5},{8,10},{9,11},{10,... | collective-permute-start | bytes 221192 | tf_op jit(solution)/shard_map/ppermute | solution.py:431
  8.0 16.5 %collective-permute-start.9 = (bf16[144,256]{1,0:T(8,128)(2,1)S(1)}, bf16[144,256]{1,0:T(8,128)(2,1)S(1)}, u32[]{:S(2)}, u32[]{:S(2)}) collective-permute-start(bf16[144,256]{1,0:T(8,128)(2,1)S(1)} %bitcast.61), channel_id=1, source_target_pairs={{0,1},{1,0},{2,3},{3,2},{4,5},{5,4},{6,7},{7,6},{8,9},{9,8},{10,11... | collective-permute-start | bytes 221192 | tf_op jit(solution)/shard_map/ppermute | solution.py:431
  8.5 0.9 %copy-start.3 = (bf16[1,2,69,256]{3,1,2,0:T(2,128)(2,1)S(1)}, bf16[1,2,69,256]{3,1,2,0:T(2,128)(2,1)}, u32[]{:S(2)}) copy-start(bf16[1,2,69,256]{3,1,2,0:T(2,128)(2,1)} %param.13) | copy-start | bytes 211972
  9.6 2.8 %copy-start.1 = (bf16[3,3,128,69]{2,3,1,0:T(8,128)(2,1)S(1)}, bf16[3,3,128,69]{2,3,1,0:T(8,128)(2,1)}, u32[]{:S(2)}) copy-start(bf16[3,3,128,69]{2,3,1,0:T(8,128)(2,1)} %param.14) | copy-start | bytes 476932
  9.7 4.4 %copy-start = (bf16[3,3,69,128]{3,2,1,0:T(8,128)(2,1)S(1)}, bf16[3,3,69,128]{3,2,1,0:T(8,128)(2,1)}, u32[]{:S(2)}) copy-start(bf16[3,3,69,128]{3,2,1,0:T(8,128)(2,1)} %param.15) | copy-start | bytes 476932
  9.7 11.4 %collective-permute-start.5 = (bf16[2,144,256]{2,1,0:T(8,128)(2,1)S(1)}, bf16[2,144,256]{2,1,0:T(8,128)(2,1)S(1)}, u32[]{:S(2)}, u32[]{:S(2)}) collective-permute-start(bf16[2,144,256]{2,1,0:T(8,128)(2,1)S(1)} %pad_maximum_fusion.6.b0), channel_id=1, source_target_pairs={{0,2},{1,3},{2,0},{3,1},{4,6},{5,7},{6,4},{7,5},{8,10},{9,11},{10,... | collective-permute-start | bytes 442376 | tf_op jit(solution)/shard_map/ppermute | solution.py:431
  12.5 7.9 %collective-permute-start.2 = (bf16[144,256]{1,0:T(8,128)(2,1)S(1)}, bf16[144,256]{1,0:T(8,128)(2,1)S(1)}, u32[]{:S(2)}, u32[]{:S(2)}) collective-permute-start(bf16[144,256]{1,0:T(8,128)(2,1)S(1)} %collective-permute-done.1.y2), channel_id=1, source_target_pairs={{0,1},{1,0},{2,3},{3,2},{4,5},{5,4},{6,7},{7,6},{8,9},{9,8},{10,11... | collective-permute-start | bytes 221192 | tf_op jit(solution)/shard_map/ppermute | solution.py:431
  14.2 12.0 %collective-permute-start.4 = (bf16[2,144,256]{2,1,0:T(8,128)(2,1)S(1)}, bf16[2,144,256]{2,1,0:T(8,128)(2,1)S(1)}, u32[]{:S(2)}, u32[]{:S(2)}) collective-permute-start(bf16[2,144,256]{2,1,0:T(8,128)(2,1)S(1)} %pad_maximum_fusion.6.b0), channel_id=1, source_target_pairs={{0,1},{1,0},{2,3},{3,2},{4,5},{5,4},{6,7},{7,6},{8,9},{9,8},{10,11... | collective-permute-start | bytes 442376 | tf_op jit(solution)/shard_map/ppermute | solution.py:431
  20.4 8.8 %collective-permute-start.3 = (bf16[4,144,256]{2,1,0:T(8,128)(2,1)S(1)}, bf16[4,144,256]{2,1,0:T(8,128)(2,1)S(1)}, u32[]{:S(2)}, u32[]{:S(2)}) collective-permute-start(bf16[4,144,256]{2,1,0:T(8,128)(2,1)S(1)} %pad_maximum_fusion.4), channel_id=1, source_target_pairs={{0,12},{4,0},{8,4},{12,8},{1,13},{5,1},{9,5},{13,9},{2,14},{6,2},{... | collective-permute-start | bytes 884744 | tf_op jit(solution)/shard_map/ppermute | solution.py:441
  20.6 5.1 %collective-permute-start.11 = (bf16[144,256]{1,0:T(8,128)(2,1)S(1)}, bf16[144,256]{1,0:T(8,128)(2,1)S(1)}, u32[]{:S(2)}, u32[]{:S(2)}) collective-permute-start(bf16[144,256]{1,0:T(8,128)(2,1)S(1)} %collective-permute-done.10.p2), channel_id=1, source_target_pairs={{0,1},{1,0},{2,3},{3,2},{4,5},{5,4},{6,7},{7,6},{8,9},{9,8},{10,11... | collective-permute-start | bytes 221192 | tf_op jit(solution)/shard_map/ppermute | solution.py:431
  21.1 7.3 %collective-permute-start.6 = (bf16[2,144,256]{2,1,0:T(8,128)(2,1)S(1)}, bf16[2,144,256]{2,1,0:T(8,128)(2,1)S(1)}, u32[]{:S(2)}, u32[]{:S(2)}) collective-permute-start(bf16[2,144,256]{2,1,0:T(8,128)(2,1)S(1)} %collective-permute-done.5.b2), channel_id=1, source_target_pairs={{0,1},{1,0},{2,3},{3,2},{4,5},{5,4},{6,7},{7,6},{8,9},{9,8},{10,11... | collective-permute-start | bytes 442376 | tf_op jit(solution)/shard_map/ppermute | solution.py:431
  23.3 0.7 %copy-start.7 = (f32[128]{0:T(128)S(1)}, f32[128]{0:T(128)}, u32[]{:S(2)}) copy-start(f32[128]{0:T(128)} %param.16) | copy-start | bytes 1540
  25.7 10.0 %collective-permute-start.12 = (bf16[4,144,256]{2,1,0:T(8,128)(2,1)S(1)}, bf16[4,144,256]{2,1,0:T(8,128)(2,1)S(1)}, u32[]{:S(2)}, u32[]{:S(2)}) collective-permute-start(bf16[4,144,256]{2,1,0:T(8,128)(2,1)S(1)} %pad_maximum_fusion.5), channel_id=1, source_target_pairs={{0,12},{4,0},{8,4},{12,8},{1,13},{5,1},{9,5},{13,9},{2,14},{6,2},{... | collective-permute-start | bytes 884744 | tf_op jit(solution)/shard_map/ppermute | solution.py:441
  30.9 5.1 %collective-permute-start.8 = (bf16[4,144,256]{2,1,0:T(8,128)(2,1)S(1)}, bf16[4,144,256]{2,1,0:T(8,128)(2,1)S(1)}, u32[]{:S(2)}, u32[]{:S(2)}) collective-permute-start(bf16[4,144,256]{2,1,0:T(8,128)(2,1)S(1)} %get-tuple-element.20), channel_id=1, source_target_pairs={{0,12},{4,0},{8,4},{12,8},{1,13},{5,1},{9,5},{13,9},{2,14},{6,2},{... | collective-permute-start | bytes 884744 | tf_op jit(solution)/shard_map/ppermute | solution.py:441
  33.0 8.5 %collective-permute-start.7 = (bf16[4,144,256]{2,1,0:T(8,128)(2,1)S(1)}, bf16[4,144,256]{2,1,0:T(8,128)(2,1)S(1)}, u32[]{:S(2)}, u32[]{:S(2)}) collective-permute-start(bf16[4,144,256]{2,1,0:T(8,128)(2,1)S(1)} %get-tuple-element.17), channel_id=1, source_target_pairs={{0,4},{4,8},{8,12},{12,0},{1,5},{5,9},{9,13},{13,1},{2,6},{6,10},{... | collective-permute-start | bytes 884744 | tf_op jit(solution)/shard_map/ppermute | solution.py:441
  41.7 4.3 %collective-permute-start.13 = (bf16[4,144,256]{2,1,0:T(8,128)(2,1)S(1)}, bf16[4,144,256]{2,1,0:T(8,128)(2,1)S(1)}, u32[]{:S(2)}, u32[]{:S(2)}) collective-permute-start(bf16[4,144,256]{2,1,0:T(8,128)(2,1)S(1)} %get-tuple-element.23), channel_id=1, source_target_pairs={{0,12},{4,0},{8,4},{12,8},{1,13},{5,1},{9,5},{13,9},{2,14},{6,2},{... | collective-permute-start | bytes 884744 | tf_op jit(solution)/shard_map/ppermute | solution.py:441
  43.0 11.3 %collective-permute-start.17 = (bf16[4,144,256]{2,1,0:T(8,128)(2,1)S(1)}, bf16[4,144,256]{2,1,0:T(8,128)(2,1)S(1)}, u32[]{:S(2)}, u32[]{:S(2)}) collective-permute-start(bf16[4,144,256]{2,1,0:T(8,128)(2,1)S(1)} %get-tuple-element.25), channel_id=1, source_target_pairs={{0,4},{4,8},{8,12},{12,0},{1,5},{5,9},{9,13},{13,1},{2,6},{6,10},{... | collective-permute-start | bytes 884744 | tf_op jit(solution)/shard_map/ppermute | solution.py:441
  46.5 7.8 %collective-permute-start.16 = (f32[8,128]{1,0:T(8,128)S(1)}, f32[8,128]{1,0:T(8,128)S(1)}, u32[]{:S(2)}, u32[]{:S(2)}) collective-permute-start(f32[8,128]{1,0:T(8,128)S(1)} %products.1.d0), channel_id=1, source_target_pairs={{0,12},{4,8},{8,4},{12,0},{1,13},{5,9},{9,5},{13,1},{2,14},{6,10},... | collective-permute-start | bytes 12296 | tf_op jit(solution)/shard_map/ppermute | solution.py:547
  48.5 6.1 %collective-permute-start.15 = (f32[8,128]{1,0:T(8,128)S(1)}, f32[8,128]{1,0:T(8,128)S(1)}, u32[]{:S(2)}, u32[]{:S(2)}) collective-permute-start(f32[8,128]{1,0:T(8,128)S(1)} %products.1.d0), channel_id=1, source_target_pairs={{0,8},{4,12},{8,0},{12,4},{1,9},{5,13},{9,1},{13,5},{2,10},{6,14},... | collective-permute-start | bytes 12296 | tf_op jit(solution)/shard_map/ppermute | solution.py:547
  52.9 1.6 %collective-permute-start.14 = (f32[8,128]{1,0:T(8,128)S(1)}, f32[8,128]{1,0:T(8,128)S(1)}, u32[]{:S(2)}, u32[]{:S(2)}) collective-permute-start(f32[8,128]{1,0:T(8,128)S(1)} %products.1.d0), channel_id=1, source_target_pairs={{0,4},{4,0},{8,12},{12,8},{1,5},{5,1},{9,13},{13,9},{2,6},{6,2},{1... | collective-permute-start | bytes 12296 | tf_op jit(solution)/shard_map/ppermute | solution.py:547
where the time goes:
time: 56.3 us; the launch traced here: 55.4 us
  starting transfers between devices  21.8 us (39%)
  Pallas kernels  14.2 us (25%)
  waiting for transfers between devices  13.8 us (25%)
  local copies, waits for them, and re-layouts  2.48 us (4%)
  between operations  1.67 us (3%)
  other arithmetic  1.49 us (3%)
    pallas_call x11, Pallas kernels, call(): pl.pallas_call(kernel, name=name, out_shape=outs, in_specs=specs, out_spe...  14.2 us
    ppermute x9, starting transfers between devices, swap(): return lax.ppermute(block, 'lat', [(i, i ^ shift) for i in range(count)])  13.3 us
    ppermute x9, waiting for transfers between devices, swap(): return lax.ppermute(block, 'lat', [(i, i ^ shift) for i in range(count)])  9.12 us
    ppermute x3, starting transfers between devices, row_plan(): lax.ppermute(dots, 'tm', [(i, i ^ step) for i in range(count)])  6.35 us
    ppermute x6, waiting for transfers between devices, along_tm(): lax.ppermute(value, 'tm', [(i, (i + step) % count) for i in range(count)])  4.44 us
    ppermute x6, starting transfers between devices, along_tm(): lax.ppermute(value, 'tm', [(i, (i + step) % count) for i in range(count)])  2.2 us
    unnamed x19, local copies, waits for them, and re-layouts  1.75 us
    convert_element_type x1, other arithmetic, as_band(): cells.astype(BF16)  1.17 us
  transfers between devices with their start and end apart: 18, of which 6 were waited for; matrix products, arithmetic and copies ran while one was open for 2% of the time, Pallas kernels for 24%

commit v1 on v0

--- a/solution.py
+++ b/solution.py
@@ -183,28 +183,51 @@
         emit(row, jnp.dot(weights, stacked, preferred_element_type=F32))
 
 
-def model_steps(field, gate, w_in, w_out, taps, hidden, count):
+def prepare(taps, hidden):
     clear_taps(taps)
     hidden[0] = jnp.zeros(hidden.shape[1:], BF16)
     hidden[ROWS + 1] = jnp.zeros(hidden.shape[1:], BF16)
 
+
+def model_step(source, target, target_b, gate, w_in, w_out, taps, hidden):
     def gated(row, value):
         hidden[row + 1] = (gate[row].astype(F32) * value).astype(BF16)
 
+    conv_rows(source, w_in, taps, gated)
+    for pair in range(BANDS):
+        stacked = hidden[2 * pair : 2 * pair + 4].reshape(-1, hidden.shape[2])
+        part = jnp.dot(w_out[...], stacked, preferred_element_type=F32)
+        lon = part.shape[1]
+        rows = []
+        for row in range(2):
+            tap = [part[(3 * row + b) * CHAN : (3 * row + b + 1) * CHAN] for b in range(3)]
+            spread = pltpu.roll(tap[0], 1, axis=1) + tap[1] + pltpu.roll(tap[2], lon - 1, axis=1)
+            rows.append(source[pair, row * CHAN : (row + 1) * CHAN, :] + spread)
+        band = jnp.concatenate(rows, axis=0)
+        target[pair] = band
+        if target_b is not None:
+            target_b[pair] = band.astype(BF16)
+
+
+def model_steps(field, gate, w_in, w_out, taps, hidden, count):
+    prepare(taps, hidden)
+
     def one_step(_, carry):
-        conv_rows(field, w_in, taps, gated)
-        for pair in range(BANDS):
-            stacked = hidden[2 * pair : 2 * pair + 4].reshape(-1, hidden.shape[2])
-            part = jnp.dot(w_out[...], stacked, preferred_element_type=F32)
-            lon = part.shape[1]
-            for row in range(2):
-                tap = [part[(3 * row + b) * CHAN : (3 * row + b + 1) * CHAN] for b in range(3)]
-                spread = pltpu.roll(tap[0], 1, axis=1) + tap[1] + pltpu.roll(tap[2], lon - 1, axis=1)
-                at = row * CHAN
-                field[pair, at : at + CHAN, :] = field[pair, at : at + CHAN, :] + spread
+        model_step(field, field, None, gate, w_in, w_out, taps, hidden)
         return carry
 
     lax.fori_loop(0, jnp.minimum(count, STEPS), one_step, 0)
+
+
+def forward_steps(start, out, out_b, gate, w_in, w_out, taps, hidden, count):
+    prepare(taps, hidden)
+    model_step(start, out, out_b, gate, w_in, w_out, taps, hidden)
+
+    def one_step(_, carry):
+        model_step(out, out, out_b, gate, w_in, w_out, taps, hidden)
+        return carry
+
+    lax.fori_loop(1, jnp.minimum(count, STEPS), one_step, 0)
 
 
 def split_16(value):
@@ -258,25 +281,28 @@
     )
 
 
-def gate_kernel(b0, b1, b2, b3, w_in, bias, gate, field, taps):
+def rhs_kernel(
+    counts,
+    y0, y1, y2, y3,
+    later,
+    b0, b1, b2, b3,
+    fore_in, bias, w_in, w_out,
+    gate, out, out_b,
+    field, taps, hidden,
+):
     me = lax.axis_index("lat")
-    for shift, block in enumerate((b0, b1, b2, b3)):
+    more = lax.axis_index("tm") < lax.axis_size("tm") - 1
+    blocks = (b0, b1, b2, b3)
+    for shift, block in enumerate(blocks):
         field[me ^ shift] = block[0].astype(F32)
-    clear_taps(taps)
+    prepare(taps, hidden)
 
     def emit(row, value):
         squashed = jnp.tanh(value + bias[...])
         gate[row] = (1.0 - squashed * squashed).astype(BF16)
 
-    conv_rows(field, w_in, taps, emit)
-
-
-def rhs_kernel(
-    counts, y0, y1, y2, y3, later, b0, b1, b2, b3, gate, w_in, w_out, out, out_b, field, taps, hidden
-):
-    me = lax.axis_index("lat")
-    more = lax.axis_index("tm") < lax.axis_size("tm") - 1
-    for shift, block in enumerate((b0, b1, b2, b3)):
+    conv_rows(field, fore_in, taps, emit)
+    for shift, block in enumerate(blocks):
         weights, slot, high, low = obs_of(block[1])
         hot = one_hot_t(slot)
         both = jnp.concatenate([hot * high, hot * low], axis=1).astype(BF16)
@@ -285,7 +311,12 @@
         )
         next_y = jnp.where(more, later[shift].astype(F32), 0.0)
         field[me ^ shift] = slots_band(slots) - next_y
-    model_steps(field, gate, w_in, w_out, taps, hidden, counts[0])
+
+    def one_step(_, carry):
+        model_step(field, field, None, gate, w_in, w_out, taps, hidden)
+        return carry
+
+    lax.fori_loop(0, jnp.minimum(counts[0], STEPS), one_step, 0)
     for shift, block in enumerate((y0, y1, y2, y3)):
         total = field[me ^ shift] + block[...].astype(F32)
         out[me ^ shift] = total
@@ -293,53 +324,71 @@
 
 
 def forward_kernel(counts, start, gate, w_in, w_out, out, out_b, taps, hidden):
-    out[...] = start[...]
-    model_steps(out, gate, w_in, w_out, taps, hidden, counts[0])
-    out_b[...] = out[...].astype(BF16)
-
-
-def observe_kernel(z, b0, b1, b2, b3, out, energy):
+    forward_steps(start, out, out_b, gate, w_in, w_out, taps, hidden, counts[0])
+
+
+def observed_band(z_band, pick, spread, weights):
+    ones = jnp.ones((2 * TILE, TILE), BF16)
+
+    def product(left, value):
+        return jnp.dot(left, jnp.concatenate(split_16(value), axis=1), preferred_element_type=F32)
+
+    picked = product(pick, band_slots(z_band))
+    terms = (picked[:, :TILE] + picked[:, TILE:]) * weights
+    terms = jnp.concatenate(split_16(terms), axis=1)
+    scaled = jnp.dot(terms, ones, preferred_element_type=F32)
+    slots = product(spread, weights * scaled)
+    squares = jnp.sum(scaled * scaled, axis=0, keepdims=True)
+    return slots_band(slots[:, :TILE] + slots[:, TILE:]), squares
+
+
+def observe_kernel(z, b0, b1, b2, b3, out, pick, spread, weights):
     me = lax.axis_index("lat")
-    squares = jnp.zeros((1, 1), F32)
     for shift, block in enumerate((b0, b1, b2, b3)):
-        weights, slot, _, _ = obs_of(block[1])
-        weights = weights.astype(F32)
-        high, low = split_16(band_slots(z[me ^ shift]))
-        both = jnp.concatenate([high, low], axis=1)
-        picked = jnp.dot(one_hot(slot).astype(BF16), both, preferred_element_type=F32)
-        picked = picked[:, :TILE] + picked[:, TILE:]
-        scaled = jnp.sum(picked * weights, axis=1, keepdims=True)
-        squares = squares + jnp.sum(scaled * scaled, axis=0, keepdims=True)
-        high, low = split_16(weights * scaled)
-        both = jnp.concatenate([high, low], axis=1)
-        slots = jnp.dot(one_hot_t(slot).astype(BF16), both, preferred_element_type=F32)
-        out[me ^ shift] = slots_band(slots[:, :TILE] + slots[:, TILE:])
+        at = me ^ shift
+        own, slot, _, _ = obs_of(block[1])
+        pick[at] = one_hot(slot).astype(BF16)
+        spread[at] = one_hot_t(slot).astype(BF16)
+        weights[at] = own.astype(F32)
+    for band in range(BANDS):
+        out[band], _ = observed_band(z[band], pick[band], spread[band], weights[band])
+
+
+def observe_again_kernel(z, pick, spread, weights, out, energy):
+    squares = jnp.zeros((1, TILE), F32)
+    for band in range(BANDS):
+        out[band], own = observed_band(z[band], pick[band], spread[band], weights[band])
+        squares = squares + own
     energy[...] = jnp.broadcast_to(squares, energy.shape)
 
 
+def next_misfit(at, shift, later, z, precision):
+    more = lax.axis_index("tm") < lax.axis_size("tm") - 1
+    weight = jnp.where(more, precision[shift].astype(F32), 0.0)
+    return later[at].astype(F32) - z[at], weight
+
+
 def adjoint_kernel(
-    counts, observed, z, later, precision, gate, w_in, w_out, out, taps, hidden
+    counts, observed, z, later, precision, gate, w_in, w_out, field, taps, hidden
 ):
     me = lax.axis_index("lat")
-    more = lax.axis_index("tm") < lax.axis_size("tm") - 1
     for shift in range(BANDS):
         at = me ^ shift
-        weight = jnp.where(more, precision[shift].astype(F32), 0.0)
-        out[at] = observed[at] - weight * (later[at].astype(F32) - z[at])
-    model_steps(out, gate, w_in, w_out, taps, hidden, counts[0])
-
-
-def image_of(at, tm_first, block, start, earlier, adjoint):
-    before = jnp.where(tm_first, 0.0, earlier[at].astype(F32))
+        misfit, weight = next_misfit(at, shift, later, z, precision)
+        field[at] = observed[at] - weight * misfit
+    model_steps(field, gate, w_in, w_out, taps, hidden, counts[0])
+
+
+def image_of(at, block, start, earlier, adjoint):
+    before = jnp.where(lax.axis_index("tm") == 0, 0.0, earlier[at].astype(F32))
     return block.astype(F32) * (start[at] - before) + adjoint[at]
 
 
 def image_kernel(start, earlier, adjoint, p0, p1, p2, p3, out, out_b):
     me = lax.axis_index("lat")
-    tm_first = lax.axis_index("tm") == 0
     for shift, block in enumerate((p0, p1, p2, p3)):
         at = me ^ shift
-        total = image_of(at, tm_first, block[...], start, earlier, adjoint)
+        total = image_of(at, block[...], start, earlier, adjoint)
         out[at] = total
         out_b[at] = total.astype(BF16)
 
@@ -347,13 +396,11 @@
 def products_kernel(first, second, z, later, precision, p0, p1, p2, p3, energy, dots):
     me = lax.axis_index("lat")
     tm_first = lax.axis_index("tm") == 0
-    more = lax.axis_index("tm") < lax.axis_size("tm") - 1
     sums = [jnp.zeros((1, first.shape[2]), F32) for _ in range(4)]
     for shift, block in enumerate((p0, p1, p2, p3)):
         at = me ^ shift
         r0, v1 = first[at], second[at]
-        misfit = later[at].astype(F32) - z[at]
-        weight = jnp.where(more, precision[shift].astype(F32), 0.0)
+        misfit, weight = next_misfit(at, shift, later, z, precision)
         initial = jnp.where(tm_first, block[...].astype(F32), 0.0)
         terms = (r0 * r0, r0 * v1, v1 * v1, weight * misfit * misfit + initial * v1 * v1)
         sums = [total + jnp.sum(term, axis=0, keepdims=True) for total, term in zip(sums, terms)]
@@ -365,7 +412,6 @@
 
 def finish_kernel(d0, d1, d2, d3, first, second, earlier, adjoint, p0, inc, res):
     me = lax.axis_index("lat")
-    tm_first = lax.axis_index("tm") == 0
     chan, _, lon = inc.shape
     total = (d0[...] + d1[...]) + (d2[...] + d3[...])
     rr0, c0, g11, g12 = [total[j : j + 1, :1] for j in range(4)]
@@ -377,7 +423,7 @@
     a1 = rr1 / c1
     wide = lambda value: jnp.broadcast_to(value, (chan, lon))
     along, cross = wide(a0 + a1 * grow), wide(a1 * a0)
-    image = image_of(me, tm_first, p0[...], second, earlier, adjoint)
+    image = image_of(me, p0[...], second, earlier, adjoint)
     r0_own, v1_own = first[me], second[me]
     for row in range(2):
         at = row * CHAN
@@ -481,7 +527,8 @@
     both_own = jnp.stack([as_band(trajectory[0]), obs_own])
     prec_own = as_band(error_precision[0])
 
-    y_all = by_partner(as_band(error_precision[0] * departures[0]))
+    y_own = as_band(error_precision[0] * departures[0])
+    y_all = [y_own, swap(y_own, 1), swap(y_own, 2), swap(y_own, 3)]
     b_all = by_partner(both_own)
     p_all = by_partner(prec_own)
     y_later = along_tm(jnp.stack(y_all), -1)
@@ -493,53 +540,65 @@
     hidden = pltpu.VMEM((ROWS + 2, hid, lon), BF16)
     field = pltpu.VMEM((BANDS, PAIR, lon), F32)
 
-    (gate,) = call(
-        gate_kernel,
-        "gate",
-        (*b_all, fore_in, hidden_bias[:, None]),
-        [shape_b(ROWS, hid, lon)],
-        [field, taps],
-    )
-    r0, r0_b = call(
+    gate_shape = shape_b(ROWS, hid, lon)
+    gate, r0, r0_b = call(
         rhs_kernel,
         "rhs",
-        (step_counts, *y_all, y_later, *b_all, gate, back_in, back_out),
-        [whole, whole_b],
+        (step_counts, *y_all, y_later, *b_all, fore_in, hidden_bias[:, None], back_in, back_out),
+        [gate_shape, whole, whole_b],
         [field, taps, hidden],
         1,
     )
-
-    def to_misfits(start, start_b):
-        later = along_tm(start_b, -1)
-        z, z_b = call(
-            forward_kernel,
-            "forward",
-            (step_counts, start, gate, fore_in, fore_out),
-            [whole, whole_b],
-            [taps, hidden],
-            1,
-        )
-        observed, energy = call(observe_kernel, "observe", (z, *b_all), [whole, shape(8, TILE)])
-        return along_tm(z_b, 1), later, z, observed, energy
-
-    def adjoint_of(later, z, observed):
-        return call(
-            adjoint_kernel,
-            "adjoint",
-            (step_counts, observed, z, later, p_later, gate, back_in, back_out),
-            [whole],
-            [taps, hidden],
-            1,
-        )[0]
-
-    earlier, later, z, observed, _ = to_misfits(r0, r0_b)
-    adjoint = adjoint_of(later, z, observed)
+    later = along_tm(r0_b, -1)
+    z1, z1_b = call(
+        forward_kernel,
+        "forward",
+        (step_counts, r0, gate, fore_in, fore_out),
+        [whole, whole_b],
+        [taps, hidden],
+        1,
+    )
+    earlier = along_tm(z1_b, 1)
+    observed, pick, spread, weights = call(
+        observe_kernel,
+        "observe",
+        (z1, *b_all),
+        [
+            whole,
+            shape_b(BANDS, 2 * TILE, SLOTS),
+            shape_b(BANDS, SLOTS, 2 * TILE),
+            shape(BANDS, 2 * TILE, TILE),
+        ],
+    )
+    (adjoint,) = call(
+        adjoint_kernel,
+        "adjoint",
+        (step_counts, observed, z1, later, p_later, gate, back_in, back_out),
+        [whole],
+        [taps, hidden],
+        1,
+    )
     v1, v1_b = call(image_kernel, "image", (r0, earlier, adjoint, *p_all), [whole, whole_b])
-    earlier, later, z, observed, energy = to_misfits(v1, v1_b)
+    later = along_tm(v1_b, -1)
+    z2, z2_b = call(
+        forward_kernel,
+        "forward",
+        (step_counts, v1, gate, fore_in, fore_out),
+        [whole, whole_b],
+        [taps, hidden],
+        1,
+    )
+    earlier = along_tm(z2_b, 1)
+    observed, energy = call(
+        observe_again_kernel,
+        "observe_again",
+        (z2, pick, spread, weights),
+        [whole, shape(8, TILE)],
+    )
     (dots,) = call(
         products_kernel,
         "products",
-        (r0, v1, z, later, p_later, *p_all, energy),
+        (r0, v1, z2, later, p_later, *p_all, energy),
         [shape(8, TILE)],
     )
     count = lax.axis_size("tm")
@@ -547,7 +606,14 @@
         lax.ppermute(dots, "tm", [(i, i ^ step) for i in range(count)]) for step in range(1, count)
     ]
     observed, _ = lax.optimization_barrier((observed, dots))
-    adjoint = adjoint_of(later, z, observed)
+    (adjoint,) = call(
+        adjoint_kernel,
+        "adjoint",
+        (step_counts, observed, z2, later, p_later, gate, back_in, back_out),
+        [whole],
+        [taps, hidden],
+        1,
+    )
     inc, res = call(
         finish_kernel,
         "finish",

time: 56.3 us -> 54.3 us (0.964); the launches traced: 55.4 us -> 54.2 us
  Pallas kernels: 14.2 us -> 18.6 us
  starting transfers between devices: 21.8 us -> 17.8 us
  waiting for transfers between devices: 13.8 us -> 11.4 us
  local copies, waits for them, and re-layouts: 2.48 us -> 3.19 us
    pallas_call x11 -> x10, Pallas kernels: 14.2 us -> 18.6 us  [call(): pl.pallas_call(kernel, name=name, out_shape=outs, in_specs=specs, out_spe...]
    ppermute x6, waiting for transfers between devices: 4.44 us -> 1.77 us  [along_tm(): lax.ppermute(value, 'tm', [(i, (i + step) % count) for i in range(count)])]
    ppermute x3, starting transfers between devices: 6.35 us -> 4.41 us  [row_plan(): lax.ppermute(dots, 'tm', [(i, i ^ step) for i in range(count)])]
    ppermute x9, starting transfers between devices: 13.3 us -> 11.6 us  [swap(): return lax.ppermute(block, 'lat', [(i, i ^ shift) for i in range(count)])]
    unnamed x19, local copies, waits for them, and re-layouts: 1.75 us -> 2.46 us
  transfers between devices with their start and end apart: 18 -> 18, of which waited for: 6 -> 5; matrix products, arithmetic and copies ran while one was open for 2% -> 2% of each run, Pallas kernels for 24% -> 32%
where the time goes in v1:
time: 54.3 us; the launch traced here: 54.2 us
  Pallas kernels  18.6 us (34%)
  starting transfers between devices  17.8 us (33%)
  waiting for transfers between devices  11.4 us (21%)
  local copies, waits for them, and re-layouts  3.19 us (6%)
  between operations  1.7 us (3%)
  other arithmetic  1.49 us (3%)
    pallas_call x10, Pallas kernels, call(): pl.pallas_call(kernel, name=name, out_shape=outs, in_specs=specs, out_spe...  18.6 us
    ppermute x9, starting transfers between devices, swap(): return lax.ppermute(block, 'lat', [(i, i ^ shift) for i in range(count)])  11.6 us
    ppermute x9, waiting for transfers between devices, swap(): return lax.ppermute(block, 'lat', [(i, i ^ shift) for i in range(count)])  9.58 us
    ppermute x3, starting transfers between devices, row_plan(): lax.ppermute(dots, 'tm', [(i, i ^ step) for i in range(count)])  4.41 us
    unnamed x19, local copies, waits for them, and re-layouts  2.46 us
    ppermute x6, starting transfers between devices, along_tm(): lax.ppermute(value, 'tm', [(i, (i + step) % count) for i in range(count)])  1.8 us
    ppermute x6, waiting for transfers between devices, along_tm(): lax.ppermute(value, 'tm', [(i, (i + step) % count) for i in range(count)])  1.77 us
    convert_element_type x1, other arithmetic, as_band(): cells.astype(BF16)  1.17 us
  transfers between devices with their start and end apart: 18, of which 5 were waited for; matrix products, arithmetic and copies ran while one was open for 2% of the time, Pallas kernels for 32%

profile of v1, /device:TPU:0, one launch (start us, length us, event | category | flops | bytes accessed | tf_op | source)
XLA Modules:
  0.0 54.2 jit_solution(1070065425666653242)
XLA Ops:
  0.6 1.2 %convert_bitcast_fusion = (bf16[2,69,256]{2,0,1:T(2,128)(2,1)S(1)}, bf16[2,69,256]{2,0,1:T(2,128)(2,1)S(1)}) fusion(f32[1,2,69,256]{3,1,2,0:T(2,128)} %param.12, f32[1,2,69,256]{3,1,2,0:T(2,128)} %param.11), kind=kLoop, calls=%fused_computation.25 | loop fusion | flops 105984 | bytes 423936 | tf_op jit(solution)/shard_map/convert_element_type | solution.py:472
  1.8 5.1 %collective-permute-start.2 = (bf16[144,256]{1,0:T(8,128)(2,1)S(1)}, bf16[144,256]{1,0:T(8,128)(2,1)S(1)}, u32[]{:S(2)}, u32[]{:S(2)}) collective-permute-start(bf16[144,256]{1,0:T(8,128)(2,1)S(1)} %bitcast.66), channel_id=1, source_target_pairs={{0,3},{1,2},{2,1},{3,0},{4,7},{5,6},{6,5},{7,4},{8,11},{9,10},{10,... | collective-permute-start | bytes 221192 | tf_op jit(solution)/shard_map/ppermute | solution.py:477
  7.0 0.6 %collective-permute-start = (bf16[144,256]{1,0:T(8,128)(2,1)S(1)}, bf16[144,256]{1,0:T(8,128)(2,1)S(1)}, u32[]{:S(2)}, u32[]{:S(2)}) collective-permute-start(bf16[144,256]{1,0:T(8,128)(2,1)S(1)} %bitcast.68), channel_id=1, source_target_pairs={{0,1},{1,0},{2,3},{3,2},{4,5},{5,4},{6,7},{7,6},{8,9},{9,8},{10,11... | collective-permute-start | bytes 221192 | tf_op jit(solution)/shard_map/ppermute | solution.py:477
  7.7 2.4 %collective-permute-start.10 = (bf16[144,256]{1,0:T(8,128)(2,1)S(1)}, bf16[144,256]{1,0:T(8,128)(2,1)S(1)}, u32[]{:S(2)}, u32[]{:S(2)}) collective-permute-start(bf16[144,256]{1,0:T(8,128)(2,1)S(1)} %bitcast.60), channel_id=1, source_target_pairs={{0,2},{1,3},{2,0},{3,1},{4,6},{5,7},{6,4},{7,5},{8,10},{9,11},{10,... | collective-permute-start | bytes 221192 | tf_op jit(solution)/shard_map/ppermute | solution.py:477
  10.0 2.0 %collective-permute-start.9 = (bf16[144,256]{1,0:T(8,128)(2,1)S(1)}, bf16[144,256]{1,0:T(8,128)(2,1)S(1)}, u32[]{:S(2)}, u32[]{:S(2)}) collective-permute-start(bf16[144,256]{1,0:T(8,128)(2,1)S(1)} %bitcast.61), channel_id=1, source_target_pairs={{0,1},{1,0},{2,3},{3,2},{4,5},{5,4},{6,7},{7,6},{8,9},{9,8},{10,11... | collective-permute-start | bytes 221192 | tf_op jit(solution)/shard_map/ppermute | solution.py:477
  12.3 0.8 %copy-done.3 = bf16[1,2,69,256]{3,1,2,0:T(2,128)(2,1)S(1)} copy-done((bf16[1,2,69,256]{3,1,2,0:T(2,128)(2,1)S(1)}, bf16[1,2,69,256]{3,1,2,0:T(2,128)(2,1)}, u32[]{:S(2)}) %copy-start.3) | copy-done | bytes 70680
  13.2 0.9 %copy-done = bf16[3,3,69,128]{3,2,1,0:T(8,128)(2,1)S(1)} copy-done((bf16[3,3,69,128]{3,2,1,0:T(8,128)(2,1)S(1)}, bf16[3,3,69,128]{3,2,1,0:T(8,128)(2,1)}, u32[]{:S(2)}) %copy-start) | copy-done | bytes 159000
  14.1 0.2 concatenate.25
  14.5 0.9 %collective-permute-done.1.y2 = bf16[144,256]{1,0:T(8,128)(2,1)S(1)} collective-permute-done((bf16[144,256]{1,0:T(8,128)(2,1)S(1)}, bf16[144,256]{1,0:T(8,128)(2,1)S(1)}, u32[]{:S(2)}, u32[]{:S(2)}) %collective-permute-start.1) | collective-permute-done | bytes 73760 | tf_op jit(solution)/shard_map/ppermute | solution.py:477
  15.6 2.4 %collective-permute-done.10.p2 = bf16[144,256]{1,0:T(8,128)(2,1)S(1)} collective-permute-done((bf16[144,256]{1,0:T(8,128)(2,1)S(1)}, bf16[144,256]{1,0:T(8,128)(2,1)S(1)}, u32[]{:S(2)}, u32[]{:S(2)}) %collective-permute-start.10) | collective-permute-done | bytes 73760 | tf_op jit(solution)/shard_map/ppermute | solution.py:477
  18.0 1.4 %collective-permute-start.11 = (bf16[144,256]{1,0:T(8,128)(2,1)S(1)}, bf16[144,256]{1,0:T(8,128)(2,1)S(1)}, u32[]{:S(2)}, u32[]{:S(2)}) collective-permute-start(bf16[144,256]{1,0:T(8,128)(2,1)S(1)} %collective-permute-done.10.p2), channel_id=1, source_target_pairs={{0,1},{1,0},{2,3},{3,2},{4,5},{5,4},{6,7},{7,6},{8,9},{9,8},{10,11... | collective-permute-start | bytes 221192 | tf_op jit(solution)/shard_map/ppermute | solution.py:477
  19.4 3.4 %collective-permute-done.5.b2 = bf16[2,144,256]{2,1,0:T(8,128)(2,1)S(1)} collective-permute-done((bf16[2,144,256]{2,1,0:T(8,128)(2,1)S(1)}, bf16[2,144,256]{2,1,0:T(8,128)(2,1)S(1)}, u32[]{:S(2)}, u32[]{:S(2)}) %collective-permute-start.5) | collective-permute-done | bytes 147488 | tf_op jit(solution)/shard_map/ppermute | solution.py:477
  23.5 0.6 %copy-done.7 = f32[128]{0:T(128)S(1)} copy-done((f32[128]{0:T(128)S(1)}, f32[128]{0:T(128)}, u32[]{:S(2)}) %copy-start.7) | copy-done | bytes 536
  24.3 0.1 copy.26.w_in
  24.4 0.1 copy.24.fore_in.w_in
  24.7 0.4 collective-permute-start.12
  25.0 2.9 %collective-permute-done.6.b3 = bf16[2,144,256]{2,1,0:T(8,128)(2,1)S(1)} collective-permute-done((bf16[2,144,256]{2,1,0:T(8,128)(2,1)S(1)}, bf16[2,144,256]{2,1,0:T(8,128)(2,1)S(1)}, u32[]{:S(2)}, u32[]{:S(2)}) %collective-permute-start.6) | collective-permute-done | bytes 147488 | tf_op jit(solution)/shard_map/ppermute | solution.py:477
  27.9 3.5 %rhs.1 = (bf16[8,128,256]{2,1,0:T(8,128)(2,1)S(1)}, f32[4,144,256]{2,1,0:T(8,128)S(1)}, bf16[4,144,256]{2,1,0:T(8,128)(2,1)S(1)}) custom-call(s32[1]{0:T(128)S(6)} %copy.36.counts, bf16[144,256]{1,0:T(8,128)(2,1)S(1)} %bitcast.70, bf16[144,256]{1,0:T(8,128)(2,1)S(1)} %collective-permute-done.y1, bf16[144,256]{1,0:T(8,128)(2,1)S(1)} %collective-permute-done.1.y2, ...), custom_call_target="tpu_custom_call" | custom-call | flops 1 | bytes 1 | tf_op jit(solution)/shard_map/rhs/pallas_call | solution.py:441
  31.4 2.4 %forward.2 = (f32[4,144,256]{2,1,0:T(8,128)S(1)}, bf16[4,144,256]{2,1,0:T(8,128)(2,1)S(1)}) custom-call(s32[1]{0:T(128)S(6)} %copy.36.counts, f32[4,144,256]{2,1,0:T(8,128)S(1)} %get-tuple-element.20.start.first, bf16[8,128,256]{2,1,0:T(8,128)(2,1)S(1)} %get-tuple-element.21.gate, bf16[128,768]{1,0:T(8,128)(2,1)S(1)} %copy.24.fore_in.w_in, ...), custom_call_target="tpu_custom_call" | custom-call | flops 1 | bytes 1 | tf_op jit(solution)/shard_map/forward/pallas_call | solution.py:441
  33.8 0.5 %collective-permute-start.7 = (bf16[4,144,256]{2,1,0:T(8,128)(2,1)S(1)}, bf16[4,144,256]{2,1,0:T(8,128)(2,1)S(1)}, u32[]{:S(2)}, u32[]{:S(2)}) collective-permute-start(bf16[4,144,256]{2,1,0:T(8,128)(2,1)S(1)} %get-tuple-element.22), channel_id=1, source_target_pairs={{0,4},{4,8},{8,12},{12,0},{1,5},{5,9},{9,13},{13,1},{2,6},{6,10},{... | collective-permute-start | bytes 884744 | tf_op jit(solution)/shard_map/ppermute | solution.py:487
  34.4 2.0 %observe.1 = (f32[4,144,256]{2,1,0:T(8,128)S(1)}, bf16[4,256,288]{2,1,0:T(8,128)(2,1)S(1)}, bf16[4,288,256]{2,1,0:T(8,128)(2,1)S(1)}, f32[4,256,128]{2,1,0:T(8,128)S(1)}) custom-call(f32[4,144,256]{2,1,0:T(8,128)S(1)} %get-tuple-element.23.z, bf16[2,144,256]{2,1,0:T(8,128)(2,1)S(1)} %pad_maximum_fusion.6.b0, ...), custom_call_target="tpu_custom_call" | custom-call | flops 1 | bytes 1 | tf_op jit(solution)/shard_map/observe/pallas_call | solution.py:441
  36.4 2.6 %adjoint.2 = f32[4,144,256]{2,1,0:T(8,128)S(1)} custom-call(s32[1]{0:T(128)S(6)} %copy.36.counts, f32[4,144,256]{2,1,0:T(8,128)S(1)} %get-tuple-element.24.observed, f32[4,144,256]{2,1,0:T(8,128)S(1)} %get-tuple-element.23.z, bf16[4,144,256]{2,1,0:T(8,128)(2,1)S(1)} %collective-permute-done.8.later, ...), custom_call_target="tpu_custom_call" | custom-call | flops 1 | bytes 1 | tf_op jit(solution)/shard_map/adjoint/pallas_call | solution.py:441
  39.0 1.8 %collective-permute-done.7.earlier = bf16[4,144,256]{2,1,0:T(8,128)(2,1)S(1)} collective-permute-done((bf16[4,144,256]{2,1,0:T(8,128)(2,1)S(1)}, bf16[4,144,256]{2,1,0:T(8,128)(2,1)S(1)}, u32[]{:S(2)}, u32[]{:S(2)}) %collective-permute-start.7) | collective-permute-done | bytes 294944 | tf_op jit(solution)/shard_map/ppermute | solution.py:487
  40.8 0.2 image.1
  41.0 2.4 %forward.3 = (f32[4,144,256]{2,1,0:T(8,128)S(1)}, bf16[4,144,256]{2,1,0:T(8,128)(2,1)S(1)}) custom-call(s32[1]{0:T(128)S(6)} %copy.36.counts, f32[4,144,256]{2,1,0:T(8,128)S(1)} %get-tuple-element.26.start.second, bf16[8,128,256]{2,1,0:T(8,128)(2,1)S(1)} %get-tuple-element.21.gate, bf16[128,768]{1,0:T(8,128)(2,1)S(1)} %copy.24.fore_in.w_in, ...), custom_call_target="tpu_custom_call" | custom-call | flops 1 | bytes 1 | tf_op jit(solution)/shard_map/forward/pallas_call | solution.py:441
  43.4 0.7 %collective-permute-start.17 = (bf16[4,144,256]{2,1,0:T(8,128)(2,1)S(1)}, bf16[4,144,256]{2,1,0:T(8,128)(2,1)S(1)}, u32[]{:S(2)}, u32[]{:S(2)}) collective-permute-start(bf16[4,144,256]{2,1,0:T(8,128)(2,1)S(1)} %get-tuple-element.33), channel_id=1, source_target_pairs={{0,4},{4,8},{8,12},{12,0},{1,5},{5,9},{9,13},{13,1},{2,6},{6,10},{... | collective-permute-start | bytes 884744 | tf_op jit(solution)/shard_map/ppermute | solution.py:487
  44.1 1.6 %observe_again.1 = (f32[4,144,256]{2,1,0:T(8,128)S(1)}, f32[8,128]{1,0:T(8,128)S(1)}) custom-call(f32[4,144,256]{2,1,0:T(8,128)S(1)} %get-tuple-element.27.z, bf16[4,256,288]{2,1,0:T(8,128)(2,1)S(1)} %get-tuple-element.29.pick, bf16[4,288,256]{2,1,0:T(8,128)(2,1)S(1)} %get-tuple-element.30.spread, f32[4,256,128]{2,1,0:T(8,128)S(1)} %get-tuple-element.31.weights), custom_call_target="tpu_custom_call" | custom-call | flops 1 | bytes 1 | tf_op jit(solution)/shard_map/observe_again/pallas_call | solution.py:441
  45.8 0.5 %products.1.d0 = f32[8,128]{1,0:T(8,128)S(1)} custom-call(f32[4,144,256]{2,1,0:T(8,128)S(1)} %get-tuple-element.20.start.first, f32[4,144,256]{2,1,0:T(8,128)S(1)} %get-tuple-element.26.start.second, f32[4,144,256]{2,1,0:T(8,128)S(1)} %get-tuple-element.27.z, bf16[4,144,256]{2,1,0:T(8,128)(2,1)S(1)} %collective-permute-done.13.later, ...), custom_call_target="tpu_custom_call" | custom-call | flops 1 | bytes 1 | tf_op jit(solution)/shard_map/products/pallas_call | solution.py:441
  46.3 1.4 %collective-permute-start.16 = (f32[8,128]{1,0:T(8,128)S(1)}, f32[8,128]{1,0:T(8,128)S(1)}, u32[]{:S(2)}, u32[]{:S(2)}) collective-permute-start(f32[8,128]{1,0:T(8,128)S(1)} %products.1.d0), channel_id=1, source_target_pairs={{0,12},{4,8},{8,4},{12,0},{1,13},{5,9},{9,5},{13,1},{2,14},{6,10},... | collective-permute-start | bytes 12296 | tf_op jit(solution)/shard_map/ppermute | solution.py:606
  47.7 3.0 %collective-permute-start.15 = (f32[8,128]{1,0:T(8,128)S(1)}, f32[8,128]{1,0:T(8,128)S(1)}, u32[]{:S(2)}, u32[]{:S(2)}) collective-permute-start(f32[8,128]{1,0:T(8,128)S(1)} %products.1.d0), channel_id=1, source_target_pairs={{0,8},{4,12},{8,0},{12,4},{1,9},{5,13},{9,1},{13,5},{2,10},{6,14},... | collective-permute-start | bytes 12296 | tf_op jit(solution)/shard_map/ppermute | solution.py:606
  50.7 2.6 %adjoint.3 = f32[4,144,256]{2,1,0:T(8,128)S(1)} custom-call(s32[1]{0:T(128)S(6)} %copy.36.counts, f32[4,144,256]{2,1,0:T(8,128)S(1)} %get-tuple-element.35.observed, f32[4,144,256]{2,1,0:T(8,128)S(1)} %get-tuple-element.27.z, bf16[4,144,256]{2,1,0:T(8,128)(2,1)S(1)} %collective-permute-done.13.later, ...), custom_call_target="tpu_custom_call" | custom-call | flops 1 | bytes 1 | tf_op jit(solution)/shard_map/adjoint/pallas_call | solution.py:441
  53.4 0.9 %finish.1 = (f32[69,2,256]{2,1,0:T(2,128)}, f32[69,2,256]{2,1,0:T(2,128)}) custom-call(f32[8,128]{1,0:T(8,128)S(1)} %products.1.d0, f32[8,128]{1,0:T(8,128)S(1)} %collective-permute-done.14.d1, f32[8,128]{1,0:T(8,128)S(1)} %collective-permute-done.15.d2, f32[8,128]{1,0:T(8,128)S(1)} %collective-permute-done.16.d3, ...), custom_call_target="tpu_custom_call" | custom-call | flops 1 | bytes 1 | tf_op jit(solution)/shard_map/finish/pallas_call | solution.py:441
  (60 shorter events, 1.1 us)
Async XLA Ops:
  1.8 12.5 %collective-permute-start.2 = (bf16[144,256]{1,0:T(8,128)(2,1)S(1)}, bf16[144,256]{1,0:T(8,128)(2,1)S(1)}, u32[]{:S(2)}, u32[]{:S(2)}) collective-permute-start(bf16[144,256]{1,0:T(8,128)(2,1)S(1)} %bitcast.66), channel_id=1, source_target_pairs={{0,3},{1,2},{2,1},{3,0},{4,7},{5,6},{6,5},{7,4},{8,11},{9,10},{10,... | collective-permute-start | bytes 221192 | tf_op jit(solution)/shard_map/ppermute | solution.py:477
  7.0 8.5 %collective-permute-start.1 = (bf16[144,256]{1,0:T(8,128)(2,1)S(1)}, bf16[144,256]{1,0:T(8,128)(2,1)S(1)}, u32[]{:S(2)}, u32[]{:S(2)}) collective-permute-start(bf16[144,256]{1,0:T(8,128)(2,1)S(1)} %bitcast.67), channel_id=1, source_target_pairs={{0,2},{1,3},{2,0},{3,1},{4,6},{5,7},{6,4},{7,5},{8,10},{9,11},{10,... | collective-permute-start | bytes 221192 | tf_op jit(solution)/shard_map/ppermute | solution.py:477
  7.0 8.5 %collective-permute-start = (bf16[144,256]{1,0:T(8,128)(2,1)S(1)}, bf16[144,256]{1,0:T(8,128)(2,1)S(1)}, u32[]{:S(2)}, u32[]{:S(2)}) collective-permute-start(bf16[144,256]{1,0:T(8,128)(2,1)S(1)} %bitcast.68), channel_id=1, source_target_pairs={{0,1},{1,0},{2,3},{3,2},{4,5},{5,4},{6,7},{7,6},{8,9},{9,8},{10,11... | collective-permute-start | bytes 221192 | tf_op jit(solution)/shard_map/ppermute | solution.py:477
  7.6 4.5 %copy-start.2 = (f32[1,256,128]{2,1,0:T(8,128)S(1)}, f32[1,256,128]{2,1,0:T(8,128)}, u32[]{:S(2)}) copy-start(f32[1,256,128]{2,1,0:T(8,128)} %param.19) | copy-start | bytes 393220
  7.6 4.4 %copy-start.6 = (s32[1,256]{1,0:T(1,128)S(1)}, s32[1,256]{1,0:T(1,128)}, u32[]{:S(2)}) copy-start(s32[1,256]{1,0:T(1,128)} %param.18) | copy-start | bytes 3076
  7.6 4.4 %copy-start.4 = (f32[1,256]{1,0:T(1,128)S(1)}, f32[1,256]{1,0:T(1,128)}, u32[]{:S(2)}) copy-start(f32[1,256]{1,0:T(1,128)} %param.20) | copy-start | bytes 3076
  7.6 4.4 %copy-start.5 = (f32[1,256]{1,0:T(1,128)S(1)}, f32[1,256]{1,0:T(1,128)}, u32[]{:S(2)}) copy-start(f32[1,256]{1,0:T(1,128)} %param.21) | copy-start | bytes 3076
  7.7 10.4 %collective-permute-start.10 = (bf16[144,256]{1,0:T(8,128)(2,1)S(1)}, bf16[144,256]{1,0:T(8,128)(2,1)S(1)}, u32[]{:S(2)}, u32[]{:S(2)}) collective-permute-start(bf16[144,256]{1,0:T(8,128)(2,1)S(1)} %bitcast.60), channel_id=1, source_target_pairs={{0,2},{1,3},{2,0},{3,1},{4,6},{5,7},{6,4},{7,5},{8,10},{9,11},{10,... | collective-permute-start | bytes 221192 | tf_op jit(solution)/shard_map/ppermute | solution.py:477
  10.0 14.6 %collective-permute-start.9 = (bf16[144,256]{1,0:T(8,128)(2,1)S(1)}, bf16[144,256]{1,0:T(8,128)(2,1)S(1)}, u32[]{:S(2)}, u32[]{:S(2)}) collective-permute-start(bf16[144,256]{1,0:T(8,128)(2,1)S(1)} %bitcast.61), channel_id=1, source_target_pairs={{0,1},{1,0},{2,3},{3,2},{4,5},{5,4},{6,7},{7,6},{8,9},{9,8},{10,11... | collective-permute-start | bytes 221192 | tf_op jit(solution)/shard_map/ppermute | solution.py:477
  12.2 0.9 %copy-start.3 = (bf16[1,2,69,256]{3,1,2,0:T(2,128)(2,1)S(1)}, bf16[1,2,69,256]{3,1,2,0:T(2,128)(2,1)}, u32[]{:S(2)}) copy-start(bf16[1,2,69,256]{3,1,2,0:T(2,128)(2,1)} %param.13) | copy-start | bytes 211972
  12.3 0.9 %copy-start.1 = (bf16[3,3,128,69]{2,3,1,0:T(8,128)(2,1)S(1)}, bf16[3,3,128,69]{2,3,1,0:T(8,128)(2,1)}, u32[]{:S(2)}) copy-start(bf16[3,3,128,69]{2,3,1,0:T(8,128)(2,1)} %param.14) | copy-start | bytes 476932
  13.2 0.9 %copy-start = (bf16[3,3,69,128]{3,2,1,0:T(8,128)(2,1)S(1)}, bf16[3,3,69,128]{3,2,1,0:T(8,128)(2,1)}, u32[]{:S(2)}) copy-start(bf16[3,3,69,128]{3,2,1,0:T(8,128)(2,1)} %param.15) | copy-start | bytes 476932
  14.3 8.4 %collective-permute-start.5 = (bf16[2,144,256]{2,1,0:T(8,128)(2,1)S(1)}, bf16[2,144,256]{2,1,0:T(8,128)(2,1)S(1)}, u32[]{:S(2)}, u32[]{:S(2)}) collective-permute-start(bf16[2,144,256]{2,1,0:T(8,128)(2,1)S(1)} %pad_maximum_fusion.6.b0), channel_id=1, source_target_pairs={{0,2},{1,3},{2,0},{3,1},{4,6},{5,7},{6,4},{7,5},{8,10},{9,11},{10,... | collective-permute-start | bytes 442376 | tf_op jit(solution)/shard_map/ppermute | solution.py:477
  15.4 9.6 %collective-permute-start.4 = (bf16[2,144,256]{2,1,0:T(8,128)(2,1)S(1)}, bf16[2,144,256]{2,1,0:T(8,128)(2,1)S(1)}, u32[]{:S(2)}, u32[]{:S(2)}) collective-permute-start(bf16[2,144,256]{2,1,0:T(8,128)(2,1)S(1)} %pad_maximum_fusion.6.b0), channel_id=1, source_target_pairs={{0,1},{1,0},{2,3},{3,2},{4,5},{5,4},{6,7},{7,6},{8,9},{9,8},{10,11... | collective-permute-start | bytes 442376 | tf_op jit(solution)/shard_map/ppermute | solution.py:477
  15.5 12.4 %collective-permute-start.3 = (bf16[4,144,256]{2,1,0:T(8,128)(2,1)S(1)}, bf16[4,144,256]{2,1,0:T(8,128)(2,1)S(1)}, u32[]{:S(2)}, u32[]{:S(2)}) collective-permute-start(bf16[4,144,256]{2,1,0:T(8,128)(2,1)S(1)} %pad_maximum_fusion.4), channel_id=1, source_target_pairs={{0,12},{4,0},{8,4},{12,8},{1,13},{5,1},{9,5},{13,9},{2,14},{6,2},{... | collective-permute-start | bytes 884744 | tf_op jit(solution)/shard_map/ppermute | solution.py:487
  18.0 6.6 %collective-permute-start.11 = (bf16[144,256]{1,0:T(8,128)(2,1)S(1)}, bf16[144,256]{1,0:T(8,128)(2,1)S(1)}, u32[]{:S(2)}, u32[]{:S(2)}) collective-permute-start(bf16[144,256]{1,0:T(8,128)(2,1)S(1)} %collective-permute-done.10.p2), channel_id=1, source_target_pairs={{0,1},{1,0},{2,3},{3,2},{4,5},{5,4},{6,7},{7,6},{8,9},{9,8},{10,11... | collective-permute-start | bytes 221192 | tf_op jit(solution)/shard_map/ppermute | solution.py:477
  22.8 5.1 %collective-permute-start.6 = (bf16[2,144,256]{2,1,0:T(8,128)(2,1)S(1)}, bf16[2,144,256]{2,1,0:T(8,128)(2,1)S(1)}, u32[]{:S(2)}, u32[]{:S(2)}) collective-permute-start(bf16[2,144,256]{2,1,0:T(8,128)(2,1)S(1)} %collective-permute-done.5.b2), channel_id=1, source_target_pairs={{0,1},{1,0},{2,3},{3,2},{4,5},{5,4},{6,7},{7,6},{8,9},{9,8},{10,11... | collective-permute-start | bytes 442376 | tf_op jit(solution)/shard_map/ppermute | solution.py:477
  23.4 0.7 %copy-start.7 = (f32[128]{0:T(128)S(1)}, f32[128]{0:T(128)}, u32[]{:S(2)}) copy-start(f32[128]{0:T(128)} %param.16) | copy-start | bytes 1540
  24.7 11.8 %collective-permute-start.12 = (bf16[4,144,256]{2,1,0:T(8,128)(2,1)S(1)}, bf16[4,144,256]{2,1,0:T(8,128)(2,1)S(1)}, u32[]{:S(2)}, u32[]{:S(2)}) collective-permute-start(bf16[4,144,256]{2,1,0:T(8,128)(2,1)S(1)} %pad_maximum_fusion.5), channel_id=1, source_target_pairs={{0,12},{4,0},{8,4},{12,8},{1,13},{5,1},{9,5},{13,9},{2,14},{6,2},{... | collective-permute-start | bytes 884744 | tf_op jit(solution)/shard_map/ppermute | solution.py:487
  31.4 5.1 %collective-permute-start.8 = (bf16[4,144,256]{2,1,0:T(8,128)(2,1)S(1)}, bf16[4,144,256]{2,1,0:T(8,128)(2,1)S(1)}, u32[]{:S(2)}, u32[]{:S(2)}) collective-permute-start(bf16[4,144,256]{2,1,0:T(8,128)(2,1)S(1)} %get-tuple-element.25), channel_id=1, source_target_pairs={{0,12},{4,0},{8,4},{12,8},{1,13},{5,1},{9,5},{13,9},{2,14},{6,2},{... | collective-permute-start | bytes 884744 | tf_op jit(solution)/shard_map/ppermute | solution.py:487
  33.8 6.9 %collective-permute-start.7 = (bf16[4,144,256]{2,1,0:T(8,128)(2,1)S(1)}, bf16[4,144,256]{2,1,0:T(8,128)(2,1)S(1)}, u32[]{:S(2)}, u32[]{:S(2)}) collective-permute-start(bf16[4,144,256]{2,1,0:T(8,128)(2,1)S(1)} %get-tuple-element.22), channel_id=1, source_target_pairs={{0,4},{4,8},{8,12},{12,0},{1,5},{5,9},{9,13},{13,1},{2,6},{6,10},{... | collective-permute-start | bytes 884744 | tf_op jit(solution)/shard_map/ppermute | solution.py:487
  41.0 4.8 %collective-permute-start.13 = (bf16[4,144,256]{2,1,0:T(8,128)(2,1)S(1)}, bf16[4,144,256]{2,1,0:T(8,128)(2,1)S(1)}, u32[]{:S(2)}, u32[]{:S(2)}) collective-permute-start(bf16[4,144,256]{2,1,0:T(8,128)(2,1)S(1)} %get-tuple-element.28), channel_id=1, source_target_pairs={{0,12},{4,0},{8,4},{12,8},{1,13},{5,1},{9,5},{13,9},{2,14},{6,2},{... | collective-permute-start | bytes 884744 | tf_op jit(solution)/shard_map/ppermute | solution.py:487
  43.4 9.9 %collective-permute-start.17 = (bf16[4,144,256]{2,1,0:T(8,128)(2,1)S(1)}, bf16[4,144,256]{2,1,0:T(8,128)(2,1)S(1)}, u32[]{:S(2)}, u32[]{:S(2)}) collective-permute-start(bf16[4,144,256]{2,1,0:T(8,128)(2,1)S(1)} %get-tuple-element.33), channel_id=1, source_target_pairs={{0,4},{4,8},{8,12},{12,0},{1,5},{5,9},{9,13},{13,1},{2,6},{6,10},{... | collective-permute-start | bytes 884744 | tf_op jit(solution)/shard_map/ppermute | solution.py:487
  46.3 7.0 %collective-permute-start.16 = (f32[8,128]{1,0:T(8,128)S(1)}, f32[8,128]{1,0:T(8,128)S(1)}, u32[]{:S(2)}, u32[]{:S(2)}) collective-permute-start(f32[8,128]{1,0:T(8,128)S(1)} %products.1.d0), channel_id=1, source_target_pairs={{0,12},{4,8},{8,4},{12,0},{1,13},{5,9},{9,5},{13,1},{2,14},{6,10},... | collective-permute-start | bytes 12296 | tf_op jit(solution)/shard_map/ppermute | solution.py:606
  47.7 5.6 %collective-permute-start.15 = (f32[8,128]{1,0:T(8,128)S(1)}, f32[8,128]{1,0:T(8,128)S(1)}, u32[]{:S(2)}, u32[]{:S(2)}) collective-permute-start(f32[8,128]{1,0:T(8,128)S(1)} %products.1.d0), channel_id=1, source_target_pairs={{0,8},{4,12},{8,0},{12,4},{1,9},{5,13},{9,1},{13,5},{2,10},{6,14},... | collective-permute-start | bytes 12296 | tf_op jit(solution)/shard_map/ppermute | solution.py:606
  50.7 2.6 %collective-permute-start.14 = (f32[8,128]{1,0:T(8,128)S(1)}, f32[8,128]{1,0:T(8,128)S(1)}, u32[]{:S(2)}, u32[]{:S(2)}) collective-permute-start(f32[8,128]{1,0:T(8,128)S(1)} %products.1.d0), channel_id=1, source_target_pairs={{0,4},{4,0},{8,12},{12,8},{1,5},{5,1},{9,13},{13,9},{2,6},{6,2},{1... | collective-permute-start | bytes 12296 | tf_op jit(solution)/shard_map/ppermute | solution.py:606
